TPU v7x, 512 devices: a whole 4x4x16 slice. The times are simulated.
512 devices in a mesh: quad: 16 (over z), slab: 32 (over y, x, core).
Axes of the slice: x: 4, y: 4, z: 16, core: 2. Of those that a mesh axis runs over, the one named last changes fastest.
Arguments:
- factors: bfloat16 [16, 32, 2, 512, 512], P('quad', 'slab'), may hold values from -0.1875 to 0.1875
- onsite: float32 [32, 512, 512], P('slab'), may hold values from -0.25 to 0.25, as said below
- coupling: float32 [32, 128, 128], P('slab'), may hold values from -1 to 1
- vectors: bfloat16 [32, 512, 128], P('slab'), may hold values from -1.5 to 1.5
- quad_weight: float32 [16, 2], P('quad'), may hold values from -0.6 to 0.6
Outputs:
- subspace: float32 [32, 512, 128], P('slab', 'quad')
- correlation: float32 [128, 128], replicated
- projected: float32 [128, 128], replicated
Inputs may be any that keep to these rules, and one draw needn't show every extreme that they name: `onsite`: each diagonal block is symmetric, and its largest entry magnitude is exactly 8 / sqrt(1024).
All inputs are finite; a program needn't handle non-finite values.
Results may differ from a plain program's by a relative error of at most 0.0003.
Values sent between devices are 32-bit elements; how exact they have to be, the bound alone decides.
No kernel may reach another device: no remote copies, remote signals or barrier semaphores. Data moves between devices by JAX's collectives and lax.ppermute only.
A program may use at most 64 MiB of HBM per device.

v0:
```python
import jax
import jax.numpy as jnp
from jax import lax
from jax.sharding import Mesh
from jax.sharding import PartitionSpec as P

SLAB = ("slab_0", "slab_1", "slab_2")


precise = lax.Precision.HIGHEST


def filled_with(x, identity):
    return jax.tree.map(
        lambda part, zero: jnp.zeros_like(part) + jnp.asarray(zero, part.dtype), x, identity
    )


def carried_in(x, axes, combine, identity, reverse):
    before = start = filled_with(x, identity)
    so_far = x
    for axis in reversed(axes):
        count, mine = (lax.axis_size(axis), lax.axis_index(axis))
        pieces = jax.tree.map(lambda part: lax.all_gather(part, axis), so_far)
        inside, so_far = (start, start)
        for k in reversed(range(count)) if reverse else range(count):
            passed = k > mine if reverse else k < mine
            so_far = combine(so_far, jax.tree.map(lambda part: part[k], pieces))
            inside = jax.tree.map(lambda new, old: jnp.where(passed, new, old), so_far, inside)
        before = combine(inside, before)
    return before


def filled_up(lines, count):
    spare = -lines.shape[0] % count
    if not spare:
        return lines
    return jnp.concatenate([lines, jnp.zeros((spare, *lines.shape[1:]), lines.dtype)])


def sent_to_all(x, axis):
    count = lax.axis_size(axis)
    return lax.all_to_all(jnp.broadcast_to(x[None], (count, *x.shape)), axis, 0, 0, tiled=True)


def joined_along(parts, dim):
    parts = jnp.moveaxis(parts, 0, dim)
    shape = parts.shape
    return parts.reshape(*shape[:dim], shape[dim] * shape[dim + 1], *shape[dim + 2 :])


def collect(x, axis, dim):
    parts = sent_to_all(x, axis)
    return joined_along(parts, dim)


def cut_along(x, dim, count):
    before, after = (x.shape[:dim], x.shape[dim + 1 :])
    return jnp.moveaxis(x.reshape(*before, count, -1, *after), dim, 0)


def summed_on_arrival(x, axis, dim):
    count = lax.axis_size(axis)
    parts = lax.all_to_all(cut_along(x, dim, count), axis, 0, 0, tiled=True)
    return jnp.sum(parts, axis=0)


def total_of(x, axes):
    lines = x.reshape(-1, x.shape[-1])
    padded = filled_up(lines, lax.axis_size(axes))
    whole = collect(summed_on_arrival(padded, axes, 0), axes, 0)
    return lax.slice_in_dim(whole, 0, len(lines)).reshape(x.shape)


def shifted(block, axis, distance):
    devices = range(lax.axis_size(axis))
    route = [(i - distance, i) for i in devices if i - distance in devices]
    return lax.ppermute(block, axis, route)


def nested_sum(x, axes):
    padded = filled_up(x, lax.axis_size(axes))
    whole = collect(summed_on_arrival(padded, axes, 0), axes, 0)
    return lax.slice_in_dim(whole, 0, len(x)).reshape(x.shape)


def packed_total(arrays, axis):
    ends = [0]
    for a in arrays:
        ends.append(ends[-1] + a.size)
    so_far = nested_sum(jnp.concatenate([a.ravel() for a in arrays]), axis)
    return tuple((so_far[b:e].reshape(a.shape) for a, b, e in zip(arrays, ends, ends[1:])))


def complex_times(left_cols, right_cols):
    real_part = jnp.dot(
        left_cols[0], right_cols[0], precision=precise, preferred_element_type=jnp.float32
    ) - jnp.dot(left_cols[1], right_cols[1], precision=precise, preferred_element_type=jnp.float32)
    imag_part = jnp.dot(
        left_cols[0], right_cols[1], precision=precise, preferred_element_type=jnp.float32
    ) + jnp.dot(left_cols[1], right_cols[0], precision=precise, preferred_element_type=jnp.float32)
    return jnp.stack([real_part, imag_part])


def real_times(real_left, right_cols):
    return jnp.stack(
        [
            jnp.dot(
                real_left, right_cols[0], precision=precise, preferred_element_type=jnp.float32
            ),
            jnp.dot(
                real_left, right_cols[1], precision=precise, preferred_element_type=jnp.float32
            ),
        ]
    )


def times_real(left_cols, real_right):
    return jnp.stack(
        [
            jnp.dot(
                left_cols[0], real_right, precision=precise, preferred_element_type=jnp.float32
            ),
            jnp.dot(
                left_cols[1], real_right, precision=precise, preferred_element_type=jnp.float32
            ),
        ]
    )


def compose(earlier, later):
    return (complex_times(later[0], earlier[0]), complex_times(later[0], earlier[1]) + later[1])


def half_plus_upper(field_rows, next_rows, onsite, coupling):
    orbitals = field_rows.shape[1]
    plane_rows = coupling.shape[1]
    half_diag = 0.5 * jnp.dot(
        onsite[0], field_rows[0], precision=precise, preferred_element_type=jnp.float32
    )
    upper_part = jnp.dot(
        coupling[0], next_rows, precision=precise, preferred_element_type=jnp.float32
    )
    pieces = [
        jnp.concatenate(
            [half_diag[: orbitals - plane_rows], half_diag[orbitals - plane_rows :] + upper_part],
            axis=0,
        )
    ]
    return jnp.stack(pieces)


def tile_sums(field_rows, weighted):
    columns = field_rows.shape[2]
    flattened = field_rows.reshape(-1, columns)
    gram_part = lax.dot_general(
        flattened,
        flattened,
        (((0,), (0,)), ((), ())),
        precision=precise,
        preferred_element_type=jnp.float32,
    )
    weighted_part = lax.dot_general(
        flattened,
        weighted.reshape(-1, columns),
        (((0,), (0,)), ((), ())),
        precision=precise,
        preferred_element_type=jnp.float32,
    )
    return (gram_part, weighted_part)


def per_device(factors, onsite, coupling, vectors, quad_weight):
    slabs_here = factors.shape[1]
    orbitals = factors.shape[3]
    columns = vectors.shape[2]
    plane_rows = coupling.shape[1]
    unit_matrix = jnp.eye(plane_rows, dtype=jnp.float32)
    identity_pair = (
        jnp.stack([unit_matrix, jnp.zeros_like(unit_matrix)]),
        jnp.zeros((2, plane_rows, columns), jnp.float32),
    )
    slab_index = 0
    factor_block = factors[0, slab_index]
    sources = [
        jnp.dot(
            factor_block.reshape(2 * orbitals, orbitals),
            vectors[slab_index],
            preferred_element_type=jnp.float32,
        ).reshape(2, orbitals, columns)
    ]
    left_cols = [factor_block[:, :, :plane_rows].astype(jnp.float32)]
    right_cols = [factor_block[:, :, orbitals - plane_rows :].astype(jnp.float32)]
    forward_map = identity_pair
    slab_index = 0
    link_t = coupling[slab_index].T
    step_map = (
        real_times(link_t, left_cols[slab_index][:, orbitals - plane_rows :]),
        real_times(link_t, sources[slab_index][:, orbitals - plane_rows :]),
    )
    forward_map = compose(forward_map, step_map)
    incoming = carried_in(forward_map, SLAB, compose, identity_pair, False)[1]
    slab_index = 0
    solved = sources[slab_index] + complex_times(left_cols[slab_index], incoming)
    partial_rows = [solved]
    backward_map = identity_pair
    for slab_index in reversed(range(slabs_here)):
        step_map = (
            times_real(right_cols[slab_index][:, :plane_rows], coupling[slab_index]),
            partial_rows[slab_index][:, :plane_rows],
        )
        backward_map = compose(backward_map, step_map)
    incoming = carried_in(backward_map, SLAB, compose, identity_pair, True)[1]
    weight = quad_weight[0]
    filtered = []
    for slab_index in reversed(range(slabs_here)):
        result = partial_rows[slab_index] + complex_times(
            right_cols[slab_index], real_times(coupling[slab_index], incoming)
        )
        incoming = result[:, :plane_rows]
        filtered.append(weight[0] * result[0] - weight[1] * result[1])
    summed = jnp.stack(filtered[::-1])
    rows_all = slabs_here * orbitals * lax.axis_size(SLAB)
    whole = total_of(summed, "quad")
    next_rows = shifted(whole[0, :plane_rows], SLAB, -1)
    weighted = half_plus_upper(whole, next_rows, onsite, coupling)
    gram_part, weighted_part = tile_sums(whole, weighted)
    gram_total, weighted_total = packed_total((gram_part, weighted_part), SLAB)
    share_rows = orbitals // lax.axis_size("quad")
    subspace = lax.dynamic_slice_in_dim(whole, lax.axis_index("quad") * share_rows, share_rows, 1)
    correlation = gram_total / rows_all
    projected = (weighted_total + weighted_total.T) / rows_all
    return (subspace, correlation, projected)


def solution(mesh):
    torus = Mesh(
        mesh.devices.reshape(mesh.shape["quad"], 4, 4, 2), ("quad", "slab_0", "slab_1", "slab_2")
    )
    return jax.shard_map(
        per_device,
        mesh=torus,
        in_specs=(
            P("quad", SLAB, None, None, None),
            P(SLAB, None, None),
            P(SLAB, None, None),
            P(SLAB, None, None),
            P("quad", None),
        ),
        out_specs=(P(SLAB, "quad", None), P(), P()),
        check_vma=False,
    )
```

profile of v0, /device:TPU:1, one launch (start us, length us, event | category | flops | bytes accessed | tf_op | source)
XLA Modules:
  0.0 280.1 jit_solution(2208066101733660658)
XLA Ops:
  0.7 1.2 fusion.109
  1.9 1.0 fusion.107
  3.7 8.5 %all-gather = f32[4,128,128]{2,1,0:T(8,128)S(1)} all-gather(f32[2,128,128]{2,1,0:T(8,128)S(1)} %pad_maximum_fusion), channel_id=2, replica_groups=mesh['quad'=16,'slab_0'=4,'slab_1'=4,'slab_2'=2] {'slab_2'}, dimensions={0}, use_global_device_ids=true | all-gather | bytes 393216 | tf_op jit(solution)/shard_map/all_gather | solution.py:24
  12.6 0.9 copy-done.110
  14.5 2.0 all_gather.68
  17.3 0.8 fusion.123
  18.1 0.8 fusion.124
  20.9 9.9 %all-gather.1 = f32[8,128,128]{2,1,0:T(8,128)S(1)} all-gather(f32[2,128,128]{2,1,0:T(8,128)S(1)} %get-tuple-element.35), channel_id=3, replica_groups=mesh['quad'=16,'slab_0'=4,'slab_1'=4,'slab_2'=2] {'slab_1'}, dimensions={0}, use_global_device_ids=true | all-gather | bytes 655360 | tf_op jit(solution)/shard_map/all_gather | solution.py:24
  32.9 11.0 %all_gather.69 = f32[4,2,128,128]{3,2,1,0:T(8,128)S(1)} all-gather(f32[1,2,128,128]{3,2,1,0:T(8,128)S(1)} %maximum_add_fusion.3), channel_id=1, replica_groups=mesh['quad'=16,'slab_0'=4,'slab_1'=4,'slab_2'=2] {'slab_1'}, dimensions={0}, use_global_device_ids=true | all-gather | bytes 655360 | tf_op jit(solution)/shard_map/all_gather | solution.py:24
  47.6 0.8 fusion.129
  48.4 0.8 fusion.130
  49.3 0.8 convolution_subtract_fusion.27
  50.1 0.8 convolution_add_fusion.28
  52.5 1.2 fusion.81
  53.7 0.8 fusion.133
  54.5 0.8 fusion.134
  58.3 9.9 %all-gather.2 = f32[8,128,128]{2,1,0:T(8,128)S(1)} all-gather(f32[2,128,128]{2,1,0:T(8,128)S(1)} %get-tuple-element.27), channel_id=4, replica_groups=mesh['quad'=16,'slab_0'=4,'slab_1'=4,'slab_2'=2] {'slab_0'}, dimensions={0}, use_global_device_ids=true | all-gather | bytes 655360 | tf_op jit(solution)/shard_map/all_gather | solution.py:24
  68.6 1.0 maximum_add_fusion.4
  69.6 9.9 %all_gather.70 = f32[4,2,128,128]{3,2,1,0:T(8,128)S(1)} all-gather(f32[1,2,128,128]{3,2,1,0:T(8,128)S(1)} %maximum_add_fusion.4), channel_id=1, replica_groups=mesh['quad'=16,'slab_0'=4,'slab_1'=4,'slab_2'=2] {'slab_0'}, dimensions={0}, use_global_device_ids=true | all-gather | bytes 655360 | tf_op jit(solution)/shard_map/all_gather | solution.py:24
  83.3 0.8 fusion.118
  84.1 0.8 fusion.117
  93.2 14.0 %all-gather.3 = f32[4,128,128]{2,1,0:T(8,128)S(1)} all-gather(f32[2,128,128]{2,1,0:T(8,128)S(1)} %pad_maximum_fusion.3), channel_id=5, replica_groups=mesh['quad'=16,'slab_0'=4,'slab_1'=4,'slab_2'=2] {'slab_2'}, dimensions={0}, use_global_device_ids=true | all-gather | bytes 393216 | tf_op jit(solution)/shard_map/all_gather | solution.py:24
  109.3 2.0 all-gather.6
  112.0 0.8 fusion.147
  112.8 0.8 fusion.148
  115.6 9.9 %all-gather.4 = f32[8,128,128]{2,1,0:T(8,128)S(1)} all-gather(f32[2,128,128]{2,1,0:T(8,128)S(1)} %get-tuple-element.23), channel_id=6, replica_groups=mesh['quad'=16,'slab_0'=4,'slab_1'=4,'slab_2'=2] {'slab_1'}, dimensions={0}, use_global_device_ids=true | all-gather | bytes 655360 | tf_op jit(solution)/shard_map/all_gather | solution.py:24
  127.6 10.9 %all_gather.79 = f32[4,2,128,128]{3,2,1,0:T(8,128)S(1)} all-gather(f32[1,2,128,128]{3,2,1,0:T(8,128)S(1)} %maximum_add_fusion.9), channel_id=1, replica_groups=mesh['quad'=16,'slab_0'=4,'slab_1'=4,'slab_2'=2] {'slab_1'}, dimensions={0}, use_global_device_ids=true | all-gather | bytes 655360 | tf_op jit(solution)/shard_map/all_gather | solution.py:24
  143.0 0.8 fusion.153
  143.9 0.8 fusion.154
  144.7 1.1 convolution_subtract_fusion.8
  145.8 1.0 convolution_add_fusion.9
  148.3 0.9 fusion.83
  149.3 0.8 fusion.157
  150.1 0.8 fusion.158
  151.3 9.9 %all_gather.80 = f32[4,2,128,128]{3,2,1,0:T(8,128)S(1)} all-gather(f32[1,2,128,128]{3,2,1,0:T(8,128)S(1)} %maximum_add_fusion.10), channel_id=1, replica_groups=mesh['quad'=16,'slab_0'=4,'slab_1'=4,'slab_2'=2] {'slab_0'}, dimensions={0}, use_global_device_ids=true | all-gather | bytes 655360 | tf_op jit(solution)/shard_map/all_gather | solution.py:24
  163.8 10.4 %all-gather.5 = f32[8,128,128]{2,1,0:T(8,128)S(1)} all-gather(f32[2,128,128]{2,1,0:T(8,128)S(1)} %get-tuple-element.15), channel_id=7, replica_groups=mesh['quad'=16,'slab_0'=4,'slab_1'=4,'slab_2'=2] {'slab_0'}, dimensions={0}, use_global_device_ids=true | all-gather | bytes 655360 | tf_op jit(solution)/shard_map/all_gather | solution.py:24
  179.0 0.8 fusion.142
  179.8 0.8 fusion.141
  189.9 1.3 fusion.51
  191.3 22.9 %all_to_all.25 = f32[16,32,128]{2,1,0:T(8,128)S(1)} all-to-all(f32[16,32,128]{2,1,0:T(8,128)S(1)} %bitcast.975), channel_id=1, replica_groups=mesh['quad'=16,'slab_0'=4,'slab_1'=4,'slab_2'=2] {'quad'}, dimensions={0} | all-to-all | bytes 524288 | tf_op jit(solution)/shard_map/all_to_all | solution.py:64
  214.2 18.3 %all_to_all.26 = f32[16,32,128]{2,1,0:T(8,128)S(1)} all-to-all(f32[16,32,128]{2,1,0:T(8,128)S(1)} %broadcast_in_dim.7), channel_id=1, replica_groups=mesh['quad'=16,'slab_0'=4,'slab_1'=4,'slab_2'=2] {'quad'}, dimensions={0} | all-to-all | bytes 524288 | tf_op jit(solution)/shard_map/all_to_all | solution.py:43
  232.5 15.7 %collective-permute-start = (f32[128,128]{1,0:T(8,128)S(1)}, f32[128,128]{1,0:T(8,128)S(1)}, u32[]{:S(2)}, u32[]{:S(2)}) collective-permute-start(f32[128,128]{1,0:T(8,128)S(1)} %slice_bitcast_fusion.27), channel_id=1, source_target_pairs={{1,0},{2,1},{3,2},{4,3},{5,4},{6,5},{7,6},{8,7},{9,8},{10,9},{11,1... | collective-permute-start | bytes 196616 | tf_op jit(solution)/shard_map/ppermute | solution.py:78
  248.3 1.3 fusion.4
  250.2 0.8 collective-permute-done
  252.0 14.2 %all_to_all.27 = f32[32,1,1024]{2,1,0:T(1,128)S(1)} all-to-all(f32[32,1,1024]{2,1,0:T(1,128)S(1)} %all_to_all.18), channel_id=1, replica_groups=mesh['quad'=16,'slab_0'=4,'slab_1'=4,'slab_2'=2] {'slab_0','slab_1','sla..., dimensions={0} | all-to-all | bytes 262144 | tf_op jit(solution)/shard_map/all_to_all | solution.py:64
  266.3 0.7 broadcast_in_dim.8
  267.0 3.9 %all-to-all-start.3 = ((f32[32,1,1024]{2,1,0:T(1,128)}), f32[32,1,1024]{2,1,0:T(1,128)S(1)}, u32[]{:S(2)}, u32[]{:S(2)}) async-start(f32[32,1,1024]{2,1,0:T(1,128)} %broadcast_in_dim.8), calls=%async_computation.3 | async-start | bytes 262144 | tf_op jit(solution)/shard_map/all_to_all | solution.py:43
  271.5 7.1 %all-to-all-done.3 = f32[32,1,1024]{2,1,0:T(1,128)S(1)} async-done(((f32[32,1,1024]{2,1,0:T(1,128)}), f32[32,1,1024]{2,1,0:T(1,128)S(1)}, u32[]{:S(2)}, u32[]{:S(2)}) %all-to-all-start.3) | async-done | bytes 131104 | tf_op jit(solution)/shard_map/all_to_all | solution.py:43
  (431 shorter events, 59.4 us)
Async XLA Ops:
  0.6 247.7 %copy-start = (f32[1,512,512]{2,1,0:T(8,128)S(1)}, f32[1,512,512]{2,1,0:T(8,128)}, u32[]{:S(2)}) copy-start(f32[1,512,512]{2,1,0:T(8,128)} %param.6) | copy-start | bytes 3145732
  0.6 1.3 copy-start.1
  0.7 11.9 %copy-start.2 = (bf16[1,1,2,512,512]{4,3,2,1,0:T(8,128)(2,1)S(1)}, bf16[1,1,2,512,512]{4,3,2,1,0:T(8,128)(2,1)}, u32[]{:S(2)}) copy-start(bf16[1,1,2,512,512]{4,3,2,1,0:T(8,128)(2,1)} %param.5) | copy-start | bytes 3145732
  12.6 0.9 copy-start.110
  17.3 1.7 copy-start.20
  30.8 0.9 copy-start.21
  31.0 1.1 copy-start.100
  31.8 12.1 %copy-start.32 = (f32[128,128]{1,0:T(8,128)}, f32[128,128]{1,0:T(8,128)S(1)}, u32[]{:S(2)}) copy-start(f32[128,128]{1,0:T(8,128)S(1)} %fusion.114) | copy-start | bytes 196612
  31.8 1.1 copy-start.11
  43.9 3.1 %copy-start.3 = (f32[4,2,128,128]{3,2,1,0:T(8,128)}, f32[4,2,128,128]{3,2,1,0:T(8,128)S(1)}, u32[]{:S(2)}) copy-start(f32[4,2,128,128]{3,2,1,0:T(8,128)S(1)} %all_gather.69) | copy-start | bytes 1572868
  50.1 0.9 copy-start.28
  51.6 0.9 copy-start.53
  68.6 10.9 %copy-start.54 = (f32[1,128,128]{2,1,0:T(8,128)}, f32[1,128,128]{2,1,0:T(8,128)S(1)}, u32[]{:S(2)}) copy-start(f32[1,128,128]{2,1,0:T(8,128)S(1)} %get-tuple-element.25) | copy-start | bytes 196612
  68.6 10.9 %copy-start.56 = (f32[1,128,128]{2,1,0:T(8,128)}, f32[1,128,128]{2,1,0:T(8,128)S(1)}, u32[]{:S(2)}) copy-start(f32[1,128,128]{2,1,0:T(8,128)S(1)} %get-tuple-element.26) | copy-start | bytes 196612
  79.5 2.8 copy-start.8
  85.0 0.9 copy-start.29
  85.0 0.9 copy-start.111
  85.0 1.1 copy-start.25
  85.0 1.1 copy-start.106
  85.0 1.3 copy-start.104
  85.2 1.6 copy-start.9
  86.5 0.9 copy-start.63
  86.6 0.9 copy-start.65
  87.5 1.0 copy-start.12
  87.8 0.9 copy-start.39
  125.5 0.9 copy-start.23
  125.7 1.1 copy-start.102
  126.5 12.0 %copy-start.34 = (f32[128,128]{1,0:T(8,128)}, f32[128,128]{1,0:T(8,128)S(1)}, u32[]{:S(2)}) copy-start(f32[128,128]{1,0:T(8,128)S(1)} %fusion.138) | copy-start | bytes 196612
  126.5 1.1 copy-start.14
  138.6 3.5 %copy-start.4 = (f32[4,2,128,128]{3,2,1,0:T(8,128)}, f32[4,2,128,128]{3,2,1,0:T(8,128)S(1)}, u32[]{:S(2)}) copy-start(f32[4,2,128,128]{3,2,1,0:T(8,128)S(1)} %all_gather.79) | copy-start | bytes 1572868
  143.9 3.0 %copy-start.30 = (f32[2,128,128]{2,1,0:T(8,128)S(1)}, f32[2,128,128]{2,1,0:T(8,128)}, u32[]{:S(2)}) copy-start(f32[2,128,128]{2,1,0:T(8,128)} %get-tuple-element.24) | copy-start | bytes 393220
  144.7 2.9 %copy-start.5 = (f32[4,2,128,128]{3,2,1,0:T(8,128)S(1)}, f32[4,2,128,128]{3,2,1,0:T(8,128)}, u32[]{:S(2)}) copy-start(f32[4,2,128,128]{3,2,1,0:T(8,128)} %copy-done.4) | copy-start | bytes 1572868
  147.4 0.9 copy-start.83
  161.2 16.7 %copy-start.6 = (f32[4,2,128,128]{3,2,1,0:T(8,128)}, f32[4,2,128,128]{3,2,1,0:T(8,128)S(1)}, u32[]{:S(2)}) copy-start(f32[4,2,128,128]{3,2,1,0:T(8,128)S(1)} %all_gather.80) | copy-start | bytes 1572868
  180.6 0.9 copy-start.31
  180.6 0.9 copy-start.112
  180.6 1.1 copy-start.27
  180.6 1.1 copy-start.107
  180.7 1.3 copy-start.105
  180.9 1.6 copy-start.7
  182.2 0.9 copy-start.71
  182.2 0.9 copy-start.73
  183.2 1.0 copy-start.15
  183.5 0.9 copy-start.43
  188.6 1.2 copy-start.17
  188.6 1.2 copy-start.19
  232.5 18.5 %collective-permute-start = (f32[128,128]{1,0:T(8,128)S(1)}, f32[128,128]{1,0:T(8,128)S(1)}, u32[]{:S(2)}, u32[]{:S(2)}) collective-permute-start(f32[128,128]{1,0:T(8,128)S(1)} %slice_bitcast_fusion.27), channel_id=1, source_target_pairs={{1,0},{2,1},{3,2},{4,3},{5,4},{6,5},{7,6},{8,7},{9,8},{10,9},{11,1... | collective-permute-start | bytes 196616 | tf_op jit(solution)/shard_map/ppermute | solution.py:78
  267.0 11.6 %all-to-all-start.3 = ((f32[32,1,1024]{2,1,0:T(1,128)}), f32[32,1,1024]{2,1,0:T(1,128)S(1)}, u32[]{:S(2)}, u32[]{:S(2)}) async-start(f32[32,1,1024]{2,1,0:T(1,128)} %broadcast_in_dim.8), calls=%async_computation.3 | async-start | bytes 262144 | tf_op jit(solution)/shard_map/all_to_all | solution.py:43
  (68 other events, 50.9 us)
where the time goes:
time: 282 us; the launch traced here: 280 us
  blocking collectives  164 us (58%)
  matrix products  51.4 us (18%)
  local copies, waits for them, and re-layouts  25.3 us (9%)
  starting transfers between devices  19.7 us (7%)
  other arithmetic  9.34 us (3%)
  waiting for transfers between devices  7.89 us (3%)
  between operations  2.84 us (1%)
    all_gather x12, blocking collectives, carried_in(): pieces = jax.tree.map(lambda part: lax.all_gather(part, axis), so_far)  108 us
    all_to_all x2, blocking collectives, summed_on_arrival(): parts = lax.all_to_all(cut_along(x, dim, count), axis, 0, 0, tiled=True)  37 us
    unnamed x228, local copies, waits for them, and re-layouts  23.1 us
    all_to_all x1, blocking collectives, sent_to_all(): lax.all_to_all(jnp.broadcast_to(x[None], (count, *x.shape)), axis, 0, 0,...  18.3 us
    ppermute x1, starting transfers between devices, shifted(): return lax.ppermute(block, axis, route)  15.7 us
    dot_general x42, matrix products, complex_times(): jnp.dot(left_cols[0], right_cols[0], precision=precise, preferred_element...  13.4 us
    dot_general x40, matrix products, complex_times(): jnp.dot(left_cols[0], right_cols[1], precision=precise, preferred_element...  13.1 us
    dot_general x38, matrix products, complex_times(): jnp.dot(left_cols[1], right_cols[1], precision=precise, preferred_element...  9.25 us
  transfers between devices with their start and end apart: 2, of which 2 were waited for; matrix products, arithmetic and copies ran while one was open for 1% of the time, Pallas kernels for 0%

commit v1 on v0

v1 whole, which is shorter than its diff:
```python
import functools

import jax
import jax.numpy as jnp
from jax import lax
from jax.experimental import pallas as pl
from jax.experimental.pallas import tpu as pltpu
from jax.sharding import Mesh
from jax.sharding import PartitionSpec as P

F32 = jnp.float32
BF16 = jnp.bfloat16
SLAB = ("y1", "y0", "x1", "x0", "core")
VMEM_BYTES = 24 << 20


def split(x):
    high = x.astype(BF16)
    return high, (x - high.astype(F32)).astype(BF16)


def dot(a, b):
    return jnp.dot(a, b, preferred_element_type=F32)


def times(left, right):
    return dot(left[0], right[0]) + (dot(left[0], right[1]) + dot(left[1], right[0]))


def wide(real, imag):
    return tuple(
        jnp.concatenate([jnp.concatenate([r, -i], 1), jnp.concatenate([i, r], 1)], 0)
        for r, i in zip(split(real), split(imag))
    )


class Pair:
    def __init__(self, get, rows):
        self.get, self.rows = get, rows

    def block(self, half, which, side):
        n = 2 * self.rows
        return self.get(half, side)[which * n : (which + 1) * n, :]

    def c_part(self, half, side):
        return self.get(half, side)[4 * self.rows : 5 * self.rows, :]

    def wide_block(self, which, side):
        m = self.block(0, which, side)
        return wide(m[: self.rows], m[self.rows :])

    def wide_c(self, side):
        return wide(self.c_part(0, side), self.c_part(1, side))


def merged(pair, half, need_a=True, need_c=True):
    start = split(pair.block(half, 0, 0))
    new_x = new_c = None
    if need_a:
        new_x = times(pair.wide_block(0, 1), start)
        if half:
            new_x = new_x + pair.block(1, 0, 1)
    z = times(pair.wide_block(1, 1), start)
    if half:
        z = z + pair.block(1, 1, 1)
    turn = pair.wide_c(0)
    new_w = pair.block(half, 1, 0) + times(turn, split(z))
    if need_c:
        rows = slice(half * pair.rows, (half + 1) * pair.rows)
        upper = jnp.concatenate([pair.c_part(0, 1), pair.c_part(1, 1)], 0)
        new_c = times((turn[0][rows], turn[1][rows]), split(upper))
    return new_x, new_w, new_c


def gathered_pair(own, other, half, rows):
    halves = (own, other) if half == 0 else (other, own)
    return Pair(lambda h, side: halves[h].at[side], rows)


def leaf_pair(own, other, half, rows):
    sides = (own, other) if half == 0 else (other, own)
    return Pair(lambda h, side: sides[side].at[h], rows)


def leaf_kernel(factor, link, vectors, out):
    rows = link.shape[0]
    last = factor.shape[1] - rows
    v, v_t = split(link[...]), split(link[...].T)
    y = vectors[...]
    for part in (0, 1):
        low, high = factor[part, :rows, :], factor[part, last:, :]
        at = slice(part * rows, (part + 1) * rows)
        left = high[:, :rows]
        out[0, at, :] = dot(v_t[0], left) + dot(v_t[1], left)
        out[1, at, :] = times(v_t, split(dot(high, y)))
        at = slice((2 + part) * rows, (3 + part) * rows)
        out[0, at, :] = low[:, :rows].astype(F32)
        out[1, at, :] = dot(low, y)
        right = low[:, last:]
        out[part, 4 * rows :, :] = dot(right, v[0]) + dot(right, v[1])


def merge_kernel(make, place, own, other, out):
    rows = out.shape[0] // 5
    for half in (0, 1):

        @pl.when(place[0] == half)
        def _():
            new_x, new_w, new_c = merged(make(own, other, half, rows), half)
            out[: 2 * rows, :] = new_x
            out[2 * rows : 4 * rows, :] = new_w
            out[4 * rows :, :] = new_c


def top_kernel(place, own, other, out):
    rows = out.shape[0] // 2

    @pl.when(place[0] == 0)
    def _():
        out[...] = merged(gathered_pair(own, other, 0, rows), 0, False, False)[1]

    @pl.when(place[0] == 1)
    def _():
        new_b, new_c, unused = merged(gathered_pair(own, other, 1, rows), 1, True, False)
        out[...] = jnp.where(place[4] == 0, new_b, new_c)


def down_kernel(place, weight, factor, link, vectors, top, *refs):
    *levels, out = refs
    rows, columns = link.shape
    orbitals = factor.shape[1]
    zero = jnp.zeros((2 * rows, columns), F32)

    def sweep(half):
        b_low, d_up, c_up = top[1, 0], top[0, 1], top[1, 1]
        mid = c_up + times(wide(d_up[:rows], d_up[rows:]), split(b_low))
        upper = place[4] == 1
        u, t = jnp.where(upper, b_low, zero), jnp.where(upper, zero, mid)
        for depth, make in ((3, gathered_pair), (2, gathered_pair), (1, gathered_pair), (0, leaf_pair)):
            own, other = levels[2 * depth], levels[2 * depth + 1]
            pair = make(own, other, half, rows)
            u_mid = times(pair.wide_block(0, 0), split(u)) + pair.block(1, 0, 0)
            t_mid = pair.block(1, 1, 1) + times(pair.wide_c(1), split(t))
            t_mid = t_mid + times(pair.wide_block(1, 1), split(u_mid))
            if depth == 0:
                u, t = (u, t_mid) if half == 0 else (u_mid, t)
            else:
                upper = place[depth] == 1
                u, t = jnp.where(upper, u_mid, u), jnp.where(upper, t, t_mid)
        w_re, w_im = weight[0, 0], weight[0, 1]
        turned = (w_re * u[:rows] - w_im * u[rows:], w_re * u[rows:] + w_im * u[:rows])
        after = (w_re * t[:rows] - w_im * t[rows:], w_re * t[rows:] + w_im * t[:rows])
        v = split(link[...])
        y = vectors[...].astype(F32)
        total = None
        for part, w in ((0, w_re), (1, -w_im)):
            sign = 1.0 if part == 0 else -1.0
            field = w * y
            moved = times(v, split(after[part]))
            field = jnp.concatenate(
                [
                    field[:rows] + sign * turned[part],
                    field[rows : orbitals - rows],
                    field[orbitals - rows :] + sign * moved,
                ],
                0,
            )
            high, low = split(field)
            f = factor[part]
            term = dot(f, high) + dot(f, low)
            total = term if total is None else total + term
        count = out.shape[0]
        share, spare = orbitals // count, rows // count
        for q in range(count):
            out[q, :share, :] = total[q * share : (q + 1) * share]
            out[q, share:, :] = after[0][q * spare : (q + 1) * spare]

    for half in (0, 1):

        @pl.when(place[0] == half)
        def _():
            sweep(half)


def tile_kernel(field, onsite, link, out):
    columns = field.shape[2]
    orbitals, rows = onsite.shape[0], link.shape[0]
    share = orbitals // field.shape[0]
    whole = field[:, :share, :].reshape(orbitals, columns)
    following = field[:, share:, :].reshape(rows, columns)
    parts = split(whole)
    weighted = 0.5 * times(split(onsite[...]), parts)
    coupled = times(split(link[...]), split(following))
    weighted = jnp.concatenate([weighted[: orbitals - rows], weighted[orbitals - rows :] + coupled], 0)
    flipped = tuple(p.T for p in parts)
    gram = times(flipped, parts)
    tile = times(flipped, split(weighted))
    tile = tile + tile.T
    row = lax.broadcasted_iota(jnp.int32, gram.shape, 0)
    col = lax.broadcasted_iota(jnp.int32, gram.shape, 1)
    packed = jnp.where(row <= col, gram, tile)
    middle = jnp.sum(jnp.where(row == col, tile, 0.0), 0, keepdims=True)
    half = columns // 2
    for h in (0, 1):
        out[h, :half, :] = packed[h * half : (h + 1) * half]
        out[h, half:, :] = jnp.broadcast_to(middle, (8, columns))


def final_kernel(scale, halves, gram_out, tile_out):
    columns = gram_out.shape[1]
    half = columns // 2
    packed = jnp.concatenate([halves[0, :half, :], halves[1, :half, :]], 0) * scale
    middle = jnp.broadcast_to(halves[0, half : half + 1, :] * scale, packed.shape)
    flipped = packed.T
    row = lax.broadcasted_iota(jnp.int32, packed.shape, 0)
    col = lax.broadcasted_iota(jnp.int32, packed.shape, 1)
    gram_out[...] = jnp.where(row <= col, packed, flipped)
    tile_out[...] = jnp.where(row == col, middle, jnp.where(row > col, packed, flipped))


SMEM = pl.BlockSpec(memory_space=pltpu.SMEM)
VMEM = pl.BlockSpec(memory_space=pltpu.VMEM)


def call(kernel, shapes, specs, *args, flops=1 << 26):
    shapes = [jax.ShapeDtypeStruct(s, F32) for s in shapes]
    single = len(shapes) == 1
    return pl.pallas_call(
        kernel,
        out_shape=shapes[0] if single else shapes,
        in_specs=specs,
        out_specs=VMEM if single else [VMEM] * len(shapes),
        compiler_params=pltpu.CompilerParams(vmem_limit_bytes=VMEM_BYTES),
        cost_estimate=pl.CostEstimate(flops=flops, bytes_accessed=1 << 20, transcendentals=0),
    )(*args)


def swapped(x):
    return lax.ppermute(x, "core", [(0, 1), (1, 0)])


def per_device(factors, onsite, coupling, vectors, quad_weight):
    factor, link, here = factors[0, 0], coupling[0], vectors[0]
    orbitals, columns = here.shape
    rows = link.shape[0]
    quads = lax.axis_size("quad")
    place = jnp.stack([lax.axis_index(a) for a in ("core", "x0", "x1", "y0", "y1")]).astype(jnp.int32)
    half_map = (5 * rows, columns)

    leaf = call(leaf_kernel, [(2, *half_map)], [VMEM] * 3, factor, link, here)
    partner = swapped(leaf)
    levels = [leaf, partner]
    mine = call(
        functools.partial(merge_kernel, leaf_pair), [half_map], [SMEM, VMEM, VMEM], place, leaf, partner
    )
    for axis in ("x0", "x1", "y0"):
        own = lax.all_gather(mine, axis)
        other = swapped(own)
        levels += [own, other]
        if axis != "y0":
            mine = call(
                functools.partial(merge_kernel, gathered_pair),
                [half_map],
                [SMEM, VMEM, VMEM],
                place,
                own,
                other,
            )
    mine = call(top_kernel, [(2 * rows, columns)], [SMEM, VMEM, VMEM], place, *levels[-2:])
    top = lax.all_gather(lax.all_gather(mine, "y1"), "core")

    share = orbitals // quads + rows // quads
    terms = call(
        down_kernel,
        [(quads, share, columns)],
        [SMEM, SMEM] + [VMEM] * (4 + len(levels)),
        place,
        quad_weight,
        factor,
        link,
        here,
        top,
        *levels,
    )
    summed = jnp.sum(lax.all_to_all(terms, "quad", 0, 0, tiled=True), axis=0)
    subspace = summed[: orbitals // quads]
    field = lax.all_to_all(
        jnp.broadcast_to(summed[None], (quads, *summed.shape)), "quad", 0, 0, tiled=True
    )
    packed = (columns // 2 + 8, columns)
    tiles = call(tile_kernel, [(2, *packed)], [VMEM] * 3, field, onsite[0], link)
    both = lax.all_gather(tiles, "core")
    core = lax.axis_index("core")
    mine = jnp.sum(lax.dynamic_index_in_dim(both, core, 1, keepdims=False), axis=0)
    plane = SLAB[:4]
    count = lax.axis_size(plane)
    spread = lax.all_to_all(jnp.broadcast_to(mine[None], (count, *packed)), plane, 0, 0, tiled=True)
    halves = lax.all_gather(jnp.sum(spread, axis=0), "core")
    scale = 1.0 / (orbitals * lax.axis_size(SLAB))
    correlation, projected = call(
        functools.partial(final_kernel, scale), [(columns, columns)] * 2, [VMEM], halves
    )
    return subspace[None], correlation, projected


def solution(mesh):
    torus = Mesh(mesh.devices.reshape(mesh.shape["quad"], 2, 2, 2, 2, 2), ("quad", *SLAB))
    return jax.shard_map(
        per_device,
        mesh=torus,
        in_specs=(
            P("quad", SLAB, None, None, None),
            P(SLAB, None, None),
            P(SLAB, None, None),
            P(SLAB, None, None),
            P("quad", None),
        ),
        out_specs=(P(SLAB, "quad", None), P(), P()),
        check_vma=False,
    )
```

time: 282 us -> 164 us (0.58)
  blocking collectives: 164 us -> 76.3 us
  matrix products: 51.4 us -> 0 us
  waiting for transfers between devices: 7.89 us -> 32.8 us
  local copies, waits for them, and re-layouts: 25.3 us -> 5.92 us
  starting transfers between devices: 19.7 us -> 36.5 us
  Pallas kernels: 0 us -> 10.9 us
  other arithmetic: 9.34 us -> 0.07 us
    all_gather x12 -> x7, blocking collectives: 108 us -> 51.5 us  [the longest x3 30.2 us: per_device(): own = lax.all_gather(mine, axis)]
    dot_general x169 -> x0, matrix products: 51.4 us -> none  [the longest x42 13.4 us: complex_times(): jnp.dot(left_cols[0], right_cols[0], precision=precise, preferred_element...]
    all_to_all x3 -> x1, blocking collectives: 55.4 us -> 24.8 us  [per_device(): summed = jnp.sum(lax.all_to_all(terms, 'quad', 0, 0, tiled=True), axis=0)]
    unnamed x228 -> x16, local copies, waits for them, and re-layouts: 23.1 us -> 3.62 us
    all_to_all x1 -> x2, waiting for transfers between devices: 7.09 us -> 26.1 us  [the longest x1 15.2 us: per_device(): lax.all_to_all(jnp.broadcast_to(summed[None], (quads, *summed.shape)), 'q...]
    all_to_all x1 -> x2, starting transfers between devices: 3.91 us -> 18.2 us  [the longest x1 11.5 us: per_device(): lax.all_to_all(jnp.broadcast_to(summed[None], (quads, *summed.shape)), 'q...]
    pallas_call x0 -> x8, Pallas kernels: none -> 10.9 us  [call(): pl.pallas_call(kernel, out_shape=shapes[0] if single else shapes, in_spec...]
    ppermute x1 -> x4, waiting for transfers between devices: 0.8 us -> 6.71 us  [swapped(): return lax.ppermute(x, 'core', [(0, 1), (1, 0)])]
  transfers between devices with their start and end apart: 2 -> 6, of which waited for: 2 -> 6; matrix products, arithmetic and copies ran while one was open for 1% -> 0% of each run, Pallas kernels for 0% -> 0%
where the time goes in v1:
time: 164 us; the launch traced here: 163 us
  blocking collectives  76.3 us (47%)
  starting transfers between devices  36.5 us (22%)
  waiting for transfers between devices  32.8 us (20%)
  Pallas kernels  10.9 us (7%)
  local copies, waits for them, and re-layouts  5.92 us (4%)
    all_gather x3, blocking collectives, per_device(): own = lax.all_gather(mine, axis)  30.2 us
    all_to_all x1, blocking collectives, per_device(): summed = jnp.sum(lax.all_to_all(terms, 'quad', 0, 0, tiled=True), axis=0)  24.8 us
    ppermute x4, starting transfers between devices, swapped(): return lax.ppermute(x, 'core', [(0, 1), (1, 0)])  18.3 us
    all_to_all x1, waiting for transfers between devices, per_device(): lax.all_to_all(jnp.broadcast_to(summed[None], (quads, *summed.shape)), 'q...  15.2 us
    all_to_all x1, starting transfers between devices, per_device(): lax.all_to_all(jnp.broadcast_to(summed[None], (quads, *summed.shape)), 'q...  11.5 us
    pallas_call x8, Pallas kernels, call(): pl.pallas_call(kernel, out_shape=shapes[0] if single else shapes, in_spec...  10.9 us
    all_to_all x1, waiting for transfers between devices, per_device(): lax.all_to_all(jnp.broadcast_to(mine[None], (count, *packed)), plane, 0,...  10.8 us
    all_gather x2, blocking collectives, per_device(): top = lax.all_gather(lax.all_gather(mine, 'y1'), 'core')  10 us
  transfers between devices with their start and end apart: 6, of which 6 were waited for; matrix products, arithmetic and copies ran while one was open for 0% of the time, Pallas kernels for 0%

profile of v1, /device:TPU:1, one launch (start us, length us, event | category | flops | bytes accessed | tf_op | source)
XLA Modules:
  0.0 163.2 jit_solution(5724831889666716205)
XLA Ops:
  0.6 0.0 copy-start
  0.6 1.2 copy-done
  1.9 0.0 copy-start.3
  1.9 0.8 copy-done.3
  2.7 0.0 copy-start.5
  2.7 0.9 copy-done.5
  3.6 0.7 shard_map.76.own.refs_0_
  4.3 8.7 %collective-permute-start = (f32[2,640,128]{2,1,0:T(8,128)S(1)}, f32[2,640,128]{2,1,0:T(8,128)S(1)}, u32[]{:S(2)}, u32[]{:S(2)}) collective-permute-start(f32[2,640,128]{2,1,0:T(8,128)S(1)} %shard_map.76.own.refs_0_), channel_id=1, source_target_pairs={{0,1},{1,0},{2,3},{3,2},{4,5},{5,4},{6,7},{7,6},{8,9},{9,8},{10,11... | collective-permute-start | bytes 1966088 | tf_op jit(solution)/shard_map/ppermute | solution.py:239
  13.1 0.1 stack.23.place
  13.2 1.6 collective-permute-done.other.refs_1_
  14.8 1.2 shard_map.77
  16.0 9.6 %all-gather = f32[1280,128]{1,0:T(8,128)S(1)} all-gather(f32[640,128]{1,0:T(8,128)S(1)} %shard_map.77), channel_id=2, replica_groups=mesh['quad'=16,'y1'=2,'y0'=2,'x1'=2,'x0'=2,'core'=2] {'x0'}, dimensions={0}, use_global_device_ids=true | all-gather | bytes 983040 | tf_op jit(solution)/shard_map/all_gather | solution.py:257
  25.6 3.1 %collective-permute-start.1 = (f32[2,640,128]{2,1,0:T(8,128)S(1)}, f32[2,640,128]{2,1,0:T(8,128)S(1)}, u32[]{:S(2)}, u32[]{:S(2)}) collective-permute-start(f32[2,640,128]{2,1,0:T(8,128)S(1)} %bitcast.18), channel_id=1, source_target_pairs={{0,1},{1,0},{2,3},{3,2},{4,5},{5,4},{6,7},{7,6},{8,9},{9,8},{10,11... | collective-permute-start | bytes 1966088 | tf_op jit(solution)/shard_map/ppermute | solution.py:239
  28.7 1.7 %collective-permute-done.1.other.refs_3_ = f32[2,640,128]{2,1,0:T(8,128)S(1)} collective-permute-done((f32[2,640,128]{2,1,0:T(8,128)S(1)}, f32[2,640,128]{2,1,0:T(8,128)S(1)}, u32[]{:S(2)}, u32[]{:S(2)}) %collective-permute-start.1) | collective-permute-done | bytes 655392 | tf_op jit(solution)/shard_map/ppermute | solution.py:239
  30.4 1.2 shard_map.78
  31.7 11.1 %all-gather.1 = f32[1280,128]{1,0:T(8,128)S(1)} all-gather(f32[640,128]{1,0:T(8,128)S(1)} %shard_map.78), channel_id=3, replica_groups=mesh['quad'=16,'y1'=2,'y0'=2,'x1'=2,'x0'=2,'core'=2] {'x1'}, dimensions={0}, use_global_device_ids=true | all-gather | bytes 983040 | tf_op jit(solution)/shard_map/all_gather | solution.py:257
  42.7 3.1 %collective-permute-start.2 = (f32[2,640,128]{2,1,0:T(8,128)S(1)}, f32[2,640,128]{2,1,0:T(8,128)S(1)}, u32[]{:S(2)}, u32[]{:S(2)}) collective-permute-start(f32[2,640,128]{2,1,0:T(8,128)S(1)} %bitcast.21), channel_id=1, source_target_pairs={{0,1},{1,0},{2,3},{3,2},{4,5},{5,4},{6,7},{7,6},{8,9},{9,8},{10,11... | collective-permute-start | bytes 1966088 | tf_op jit(solution)/shard_map/ppermute | solution.py:239
  45.9 1.7 %collective-permute-done.2.other.refs_5_ = f32[2,640,128]{2,1,0:T(8,128)S(1)} collective-permute-done((f32[2,640,128]{2,1,0:T(8,128)S(1)}, f32[2,640,128]{2,1,0:T(8,128)S(1)}, u32[]{:S(2)}, u32[]{:S(2)}) %collective-permute-start.2) | collective-permute-done | bytes 655392 | tf_op jit(solution)/shard_map/ppermute | solution.py:239
  47.6 1.2 shard_map.79
  48.8 9.6 %all-gather.2 = f32[1280,128]{1,0:T(8,128)S(1)} all-gather(f32[640,128]{1,0:T(8,128)S(1)} %shard_map.79), channel_id=4, replica_groups=mesh['quad'=16,'y1'=2,'y0'=2,'x1'=2,'x0'=2,'core'=2] {'y0'}, dimensions={0}, use_global_device_ids=true | all-gather | bytes 983040 | tf_op jit(solution)/shard_map/all_gather | solution.py:257
  58.4 0.0 copy-start.1
  58.4 3.3 %collective-permute-start.3 = (f32[2,640,128]{2,1,0:T(8,128)S(1)}, f32[2,640,128]{2,1,0:T(8,128)S(1)}, u32[]{:S(2)}, u32[]{:S(2)}) collective-permute-start(f32[2,640,128]{2,1,0:T(8,128)S(1)} %bitcast.24), channel_id=1, source_target_pairs={{0,1},{1,0},{2,3},{3,2},{4,5},{5,4},{6,7},{7,6},{8,9},{9,8},{10,11... | collective-permute-start | bytes 1966088 | tf_op jit(solution)/shard_map/ppermute | solution.py:239
  61.7 1.7 %collective-permute-done.3.other.refs_7_ = f32[2,640,128]{2,1,0:T(8,128)S(1)} collective-permute-done((f32[2,640,128]{2,1,0:T(8,128)S(1)}, f32[2,640,128]{2,1,0:T(8,128)S(1)}, u32[]{:S(2)}, u32[]{:S(2)}) %collective-permute-start.3) | collective-permute-done | bytes 655392 | tf_op jit(solution)/shard_map/ppermute | solution.py:239
  63.4 1.2 shard_map.80
  64.6 7.0 %all-gather.3 = f32[512,128]{1,0:T(8,128)S(1)} all-gather(f32[256,128]{1,0:T(8,128)S(1)} %shard_map.80), channel_id=5, replica_groups=mesh['quad'=16,'y1'=2,'y0'=2,'x1'=2,'x0'=2,'core'=2] {'y1'}, dimensions={0}, use_global_device_ids=true | all-gather | bytes 393216 | tf_op jit(solution)/shard_map/all_gather | solution.py:270
  71.5 0.0 copy-start.4
  71.5 0.0 copy-start.6
  71.5 3.1 %all-gather.4 = f32[4,256,128]{2,1,0:T(8,128)S(1)} all-gather(f32[2,256,128]{2,1,0:T(8,128)S(1)} %bitcast.37), channel_id=6, replica_groups=mesh['quad'=16,'y1'=2,'y0'=2,'x1'=2,'x0'=2,'core'=2] {'core'}, dimensions={0}, use_global_device_ids=true | all-gather | bytes 786432 | tf_op jit(solution)/shard_map/all_gather | solution.py:270
  74.6 0.0 copy-start.7
  74.6 0.0 copy-done.1
  74.6 0.0 copy-done.4
  74.6 0.0 copy-done.6
  74.6 0.6 copy-done.7
  75.2 3.3 %shard_map.81 = f32[16,40,128]{2,1,0:T(8,128)S(1)} custom-call(s32[5]{0:T(128)S(1)} %stack.23.place, f32[1,2]{1,0:T(1,128)S(1)} %copy-done.7, bf16[2,512,512]{2,1,0:T(8,128)(2,1)S(1)} %bitcast.28, f32[128,128]{1,0:T(8,128)S(1)} %bitcast.32, bf16[512,128]{1,0:T(8,128)(2,1)S(1)} %bitcast.35, f32[2,2,256,128]{3,2,1,0:T(8,128)S(1)} %bitcast.29, ...), custom_call_target="tpu_custom_call" | custom-call | flops 67108864 | bytes 1048576 | tf_op jit(solution)/shard_map/pallas_call | solution.py:228
  78.6 0.0 copy-start.2
  78.6 24.8 %all_to_all.15 = f32[16,40,128]{2,1,0:T(8,128)S(1)} all-to-all(f32[16,40,128]{2,1,0:T(8,128)S(1)} %shard_map.81), channel_id=1, replica_groups=mesh['quad'=16,'y1'=2,'y0'=2,'x1'=2,'x0'=2,'core'=2] {'quad'}, dimensions={0} | all-to-all | bytes 655360 | tf_op jit(solution)/shard_map/all_to_all | solution.py:285
  103.4 0.7 broadcast_in_dim.7
  104.2 11.5 %all-to-all-start.1 = ((f32[16,40,128]{2,1,0:T(8,128)}), f32[16,40,128]{2,1,0:T(8,128)S(1)}, u32[]{:S(2)}, u32[]{:S(2)}) async-start(f32[16,40,128]{2,1,0:T(8,128)} %broadcast_in_dim.7), calls=%async_computation.1 | async-start | bytes 655360 | tf_op jit(solution)/shard_map/all_to_all | solution.py:287
  115.7 15.2 %all-to-all-done.1.field = f32[16,40,128]{2,1,0:T(8,128)S(1)} async-done(((f32[16,40,128]{2,1,0:T(8,128)}), f32[16,40,128]{2,1,0:T(8,128)S(1)}, u32[]{:S(2)}, u32[]{:S(2)}) %all-to-all-start.1) | async-done | bytes 327712 | tf_op jit(solution)/shard_map/all_to_all | solution.py:287
  130.9 0.0 copy-done.2
  130.9 1.2 shard_map.82
  132.1 8.0 %all-gather.5 = f32[4,72,128]{2,1,0:T(8,128)S(1)} all-gather(f32[2,72,128]{2,1,0:T(8,128)S(1)} %shard_map.82), channel_id=7, replica_groups=mesh['quad'=16,'y1'=2,'y0'=2,'x1'=2,'x0'=2,'core'=2] {'core'}, dimensions={0}, use_global_device_ids=true | all-gather | bytes 221184 | tf_op jit(solution)/shard_map/all_gather | solution.py:292
  140.1 0.9 broadcast_in_dim.8
  140.9 6.8 %all-to-all-start.2 = ((f32[16,72,128]{2,1,0:T(8,128)}), f32[16,72,128]{2,1,0:T(8,128)S(1)}, u32[]{:S(2)}, u32[]{:S(2)}) async-start(f32[16,72,128]{2,1,0:T(8,128)} %broadcast_in_dim.8), calls=%async_computation.2 | async-start | bytes 1179648 | tf_op jit(solution)/shard_map/all_to_all | solution.py:297
  147.7 0.6 slice_bitcast_fusion
  148.3 10.8 %all-to-all-done.2 = f32[16,72,128]{2,1,0:T(8,128)S(1)} async-done(((f32[16,72,128]{2,1,0:T(8,128)}), f32[16,72,128]{2,1,0:T(8,128)S(1)}, u32[]{:S(2)}, u32[]{:S(2)}) %all-to-all-start.2) | async-done | bytes 589856 | tf_op jit(solution)/shard_map/all_to_all | solution.py:297
  159.2 3.3 %all-gather.6 = f32[144,128]{1,0:T(8,128)S(1)} all-gather(f32[72,128]{1,0:T(8,128)S(1)} %reduce_sum.29), channel_id=8, replica_groups=mesh['quad'=16,'y1'=2,'y0'=2,'x1'=2,'x0'=2,'core'=2] {'core'}, dimensions={0}, use_global_device_ids=true | all-gather | bytes 110592 | tf_op jit(solution)/shard_map/all_gather | solution.py:298
  162.5 0.8 shard_map.83
  (3 shorter events, 0.1 us)
Async XLA Ops:
  0.6 1.2 copy-start
  1.9 0.8 copy-start.3
  2.7 0.9 copy-start.5
  4.3 10.5 %collective-permute-start = (f32[2,640,128]{2,1,0:T(8,128)S(1)}, f32[2,640,128]{2,1,0:T(8,128)S(1)}, u32[]{:S(2)}, u32[]{:S(2)}) collective-permute-start(f32[2,640,128]{2,1,0:T(8,128)S(1)} %shard_map.76.own.refs_0_), channel_id=1, source_target_pairs={{0,1},{1,0},{2,3},{3,2},{4,5},{5,4},{6,7},{7,6},{8,9},{9,8},{10,11... | collective-permute-start | bytes 1966088 | tf_op jit(solution)/shard_map/ppermute | solution.py:239
  25.6 4.8 %collective-permute-start.1 = (f32[2,640,128]{2,1,0:T(8,128)S(1)}, f32[2,640,128]{2,1,0:T(8,128)S(1)}, u32[]{:S(2)}, u32[]{:S(2)}) collective-permute-start(f32[2,640,128]{2,1,0:T(8,128)S(1)} %bitcast.18), channel_id=1, source_target_pairs={{0,1},{1,0},{2,3},{3,2},{4,5},{5,4},{6,7},{7,6},{8,9},{9,8},{10,11... | collective-permute-start | bytes 1966088 | tf_op jit(solution)/shard_map/ppermute | solution.py:239
  42.7 4.8 %collective-permute-start.2 = (f32[2,640,128]{2,1,0:T(8,128)S(1)}, f32[2,640,128]{2,1,0:T(8,128)S(1)}, u32[]{:S(2)}, u32[]{:S(2)}) collective-permute-start(f32[2,640,128]{2,1,0:T(8,128)S(1)} %bitcast.21), channel_id=1, source_target_pairs={{0,1},{1,0},{2,3},{3,2},{4,5},{5,4},{6,7},{7,6},{8,9},{9,8},{10,11... | collective-permute-start | bytes 1966088 | tf_op jit(solution)/shard_map/ppermute | solution.py:239
  58.4 16.2 %copy-start.1 = (bf16[1,1,2,512,512]{4,3,2,1,0:T(8,128)(2,1)S(1)}, bf16[1,1,2,512,512]{4,3,2,1,0:T(8,128)(2,1)}, u32[]{:S(2)}) copy-start(bf16[1,1,2,512,512]{4,3,2,1,0:T(8,128)(2,1)} %param.5) | copy-start | bytes 3145732
  58.4 5.0 %collective-permute-start.3 = (f32[2,640,128]{2,1,0:T(8,128)S(1)}, f32[2,640,128]{2,1,0:T(8,128)S(1)}, u32[]{:S(2)}, u32[]{:S(2)}) collective-permute-start(f32[2,640,128]{2,1,0:T(8,128)S(1)} %bitcast.24), channel_id=1, source_target_pairs={{0,1},{1,0},{2,3},{3,2},{4,5},{5,4},{6,7},{7,6},{8,9},{9,8},{10,11... | collective-permute-start | bytes 1966088 | tf_op jit(solution)/shard_map/ppermute | solution.py:239
  71.5 3.1 %copy-start.4 = (f32[1,128,128]{2,1,0:T(8,128)S(1)}, f32[1,128,128]{2,1,0:T(8,128)}, u32[]{:S(2)}) copy-start(f32[1,128,128]{2,1,0:T(8,128)} %param.7) | copy-start | bytes 196612
  71.5 3.1 %copy-start.6 = (bf16[1,512,128]{2,1,0:T(8,128)(2,1)S(1)}, bf16[1,512,128]{2,1,0:T(8,128)(2,1)}, u32[]{:S(2)}) copy-start(bf16[1,512,128]{2,1,0:T(8,128)(2,1)} %param.8) | copy-start | bytes 393220
  74.6 0.7 copy-start.7
  78.6 52.3 %copy-start.2 = (f32[1,512,512]{2,1,0:T(8,128)S(1)}, f32[1,512,512]{2,1,0:T(8,128)}, u32[]{:S(2)}) copy-start(f32[1,512,512]{2,1,0:T(8,128)} %param.6) | copy-start | bytes 3145732
  104.2 26.7 %all-to-all-start.1 = ((f32[16,40,128]{2,1,0:T(8,128)}), f32[16,40,128]{2,1,0:T(8,128)S(1)}, u32[]{:S(2)}, u32[]{:S(2)}) async-start(f32[16,40,128]{2,1,0:T(8,128)} %broadcast_in_dim.7), calls=%async_computation.1 | async-start | bytes 655360 | tf_op jit(solution)/shard_map/all_to_all | solution.py:287
  140.9 18.2 %all-to-all-start.2 = ((f32[16,72,128]{2,1,0:T(8,128)}), f32[16,72,128]{2,1,0:T(8,128)S(1)}, u32[]{:S(2)}, u32[]{:S(2)}) async-start(f32[16,72,128]{2,1,0:T(8,128)} %broadcast_in_dim.8), calls=%async_computation.2 | async-start | bytes 1179648 | tf_op jit(solution)/shard_map/all_to_all | solution.py:297

commit v2 on v1

v2 whole, which is shorter than its diff:
```python
import functools

import jax
import jax.numpy as jnp
from jax import lax
from jax.experimental import pallas as pl
from jax.experimental.pallas import tpu as pltpu
from jax.sharding import Mesh
from jax.sharding import PartitionSpec as P

F32 = jnp.float32
BF16 = jnp.bfloat16
SLAB = ("y", "x", "core")
VMEM_BYTES = 24 << 20


def split(x):
    high = x.astype(BF16)
    return high, (x - high.astype(F32)).astype(BF16)


def dot(a, b):
    return jnp.dot(a, b, preferred_element_type=F32)


def times(left, right):
    return dot(left[0], right[0]) + (dot(left[0], right[1]) + dot(left[1], right[0]))


def wide(real, imag):
    return tuple(
        jnp.concatenate([jnp.concatenate([r, -i], 1), jnp.concatenate([i, r], 1)], 0)
        for r, i in zip(split(real), split(imag))
    )


class Run:
    def __init__(self, get, count, rows):
        self.get, self.count, self.rows = get, count, rows

    def block(self, half, which, k):
        n = 2 * self.rows
        return self.get(half, k)[which * n : (which + 1) * n, :]

    def c_part(self, half, k):
        return self.get(half, k)[4 * self.rows : 5 * self.rows, :]

    def wide_block(self, which, k):
        m = self.block(0, which, k)
        return wide(m[: self.rows], m[self.rows :])

    def wide_c(self, k):
        return wide(self.c_part(0, k), self.c_part(1, k))


def merged(run, half):
    states = [run.block(half, 0, 0)]
    for k in range(1, run.count):
        state = times(run.wide_block(0, k), split(states[-1]))
        states.append(state + run.block(1, 0, k) if half else state)

    def from_left(k):
        term = times(run.wide_block(1, k), split(states[k - 1]))
        return term + run.block(1, 1, k) if half else term

    last = run.count - 1
    back, turn = from_left(last), jnp.concatenate([run.c_part(0, last), run.c_part(1, last)], 0)
    columns = back.shape[1]
    for k in range(last - 1, 0, -1):
        both = times(run.wide_c(k), split(jnp.concatenate([back, turn], 1)))
        back, turn = both[:, :columns] + from_left(k), both[:, columns:]
    first = run.wide_c(0)
    back = run.block(half, 1, 0) + times(first, split(back))
    rows = slice(half * run.rows, (half + 1) * run.rows)
    return states[-1], back, times((first[0][rows], first[1][rows]), split(turn))


def entering(run, u, t):
    lefts, rights = [u], [t]
    for k in range(run.count - 1):
        b = run.block(1, 0, k)
        lefts.append(b if lefts[-1] is None else b + times(run.wide_block(0, k), split(lefts[-1])))
    for k in range(run.count - 1, 0, -1):
        term = run.block(1, 1, k) + times(run.wide_block(1, k), split(lefts[k]))
        rights.append(term if rights[-1] is None else term + times(run.wide_c(k), split(rights[-1])))
    return lefts, rights[::-1]


def chosen(options, index):
    result = options[0]
    for k, option in enumerate(options[1:], 1):
        result = jnp.where(index == k, option, result)
    return result


def gathered_run(own, other, half, rows):
    halves = (own, other) if half == 0 else (other, own)
    return Run(lambda h, k: halves[h].at[k], own.shape[0], rows)


def leaf_run(own, other, half, rows):
    sides = (own, other) if half == 0 else (other, own)
    return Run(lambda h, k: sides[k].at[h], 2, rows)


def leaf_kernel(factor, link, vectors, out, tops, bottoms, link_here, vectors_here, sems):
    rows, orbitals = link.shape[0], factor.shape[1]
    last = orbitals - rows
    copies = [
        pltpu.make_async_copy(link, link_here, sems.at[0]),
        pltpu.make_async_copy(vectors, vectors_here, sems.at[1]),
    ]
    for part in (0, 1):
        copies.append(
            pltpu.make_async_copy(factor.at[part, pl.ds(0, rows)], tops.at[part], sems.at[2 + part])
        )
        copies.append(
            pltpu.make_async_copy(factor.at[part, pl.ds(last, rows)], bottoms.at[part], sems.at[4 + part])
        )
    for copy in copies:
        copy.start()
    for copy in copies:
        copy.wait()
    v, v_t = split(link_here[...]), split(link_here[...].T)
    y = vectors_here[...]
    for part in (0, 1):
        low, high = tops[part], bottoms[part]
        at = slice(part * rows, (part + 1) * rows)
        left = high[:, :rows]
        out[0, at, :] = dot(v_t[0], left) + dot(v_t[1], left)
        out[1, at, :] = times(v_t, split(dot(high, y)))
        at = slice((2 + part) * rows, (3 + part) * rows)
        out[0, at, :] = low[:, :rows].astype(F32)
        out[1, at, :] = dot(low, y)
        right = low[:, last:]
        out[part, 4 * rows :, :] = dot(right, v[0]) + dot(right, v[1])


def merge_kernel(make, place, own, other, out):
    rows = out.shape[1] // 5
    for half in (0, 1):

        @pl.when(place[0] == half)
        def _():
            new_x, new_w, new_c = merged(make(own, other, half, rows), half)
            for k in range(out.shape[0]):
                out[k, : 2 * rows, :] = new_x
                out[k, 2 * rows : 4 * rows, :] = new_w
                out[k, 4 * rows :, :] = new_c


def down_kernel(place, weight, factor, link, vectors, leaf, leaf_2, rank, rank_2, file, file_2, out):
    rows, columns = link.shape
    orbitals = factor.shape[1]
    zero = jnp.zeros((2 * rows, columns), F32)

    def sweep(half):
        lefts, rights = entering(gathered_run(file, file_2, half, rows), None, None)
        u, t = chosen([zero] + lefts[1:], place[2]), chosen(rights[:-1] + [zero], place[2])
        lefts, rights = entering(gathered_run(rank, rank_2, half, rows), u, t)
        u, t = chosen(lefts, place[1]), chosen(rights, place[1])
        lefts, rights = entering(leaf_run(leaf, leaf_2, half, rows), u, t)
        u, t = lefts[half], rights[half]
        w_re, w_im = weight[0, 0], weight[0, 1]
        turned = (w_re * u[:rows] - w_im * u[rows:], w_re * u[rows:] + w_im * u[:rows])
        after = (w_re * t[:rows] - w_im * t[rows:], w_re * t[rows:] + w_im * t[:rows])
        v = split(link[...])
        y = vectors[...].astype(F32)
        total = None
        for part, w in ((0, w_re), (1, -w_im)):
            sign = 1.0 if part == 0 else -1.0
            field = w * y
            moved = times(v, split(after[part]))
            field = jnp.concatenate(
                [
                    field[:rows] + sign * turned[part],
                    field[rows : orbitals - rows],
                    field[orbitals - rows :] + sign * moved,
                ],
                0,
            )
            high, low = split(field)
            f = factor[part]
            term = dot(f, high) + dot(f, low)
            total = term if total is None else total + term
        count = out.shape[0]
        share, spare = orbitals // count, rows // count
        for q in range(count):
            out[q, :share, :] = total[q * share : (q + 1) * share]
            out[q, share:, :] = after[0][q * spare : (q + 1) * spare]

    for half in (0, 1):

        @pl.when(place[0] == half)
        def _():
            sweep(half)


def sum_kernel(terms, spread, share_out):
    total = jnp.sum(terms[...], 0)
    for q in range(spread.shape[0]):
        spread[q] = total
    share_out[...] = total[: share_out.shape[0]]


def pair_kernel(place, both, spread):
    total = both[0, place[0]] + both[1, place[0]]
    for k in range(spread.shape[0]):
        spread[k] = total


def tile_kernel(field, onsite, link, out):
    columns = field.shape[2]
    orbitals, rows = onsite.shape[0], link.shape[0]
    share = orbitals // field.shape[0]
    whole = field[:, :share, :].reshape(orbitals, columns)
    following = field[:, share:, :].reshape(rows, columns)
    parts = split(whole)
    weighted = 0.5 * times(split(onsite[...]), parts)
    coupled = times(split(link[...]), split(following))
    weighted = jnp.concatenate([weighted[: orbitals - rows], weighted[orbitals - rows :] + coupled], 0)
    flipped = tuple(p.T for p in parts)
    gram = times(flipped, parts)
    tile = times(flipped, split(weighted))
    tile = tile + tile.T
    row = lax.broadcasted_iota(jnp.int32, gram.shape, 0)
    col = lax.broadcasted_iota(jnp.int32, gram.shape, 1)
    packed = jnp.where(row <= col, gram, tile)
    middle = jnp.sum(jnp.where(row == col, tile, 0.0), 0, keepdims=True)
    half = columns // 2
    for h in (0, 1):
        out[h, :half, :] = packed[h * half : (h + 1) * half]
        out[h, half:, :] = jnp.broadcast_to(middle, (8, columns))


def final_kernel(scale, halves, gram_out, tile_out):
    columns = gram_out.shape[1]
    half = columns // 2
    packed = jnp.concatenate([halves[0, :half, :], halves[1, :half, :]], 0) * scale
    middle = jnp.broadcast_to(halves[0, half : half + 1, :] * scale, packed.shape)
    flipped = packed.T
    row = lax.broadcasted_iota(jnp.int32, packed.shape, 0)
    col = lax.broadcasted_iota(jnp.int32, packed.shape, 1)
    gram_out[...] = jnp.where(row <= col, packed, flipped)
    tile_out[...] = jnp.where(row == col, middle, jnp.where(row > col, packed, flipped))


SMEM = pl.BlockSpec(memory_space=pltpu.SMEM)
VMEM = pl.BlockSpec(memory_space=pltpu.VMEM)
ANY = pl.BlockSpec(memory_space=pltpu.HBM)


def call(kernel, shapes, specs, *args, scratch=(), room=VMEM_BYTES):
    shapes = [jax.ShapeDtypeStruct(s, F32) for s in shapes]
    single = len(shapes) == 1
    return pl.pallas_call(
        kernel,
        out_shape=shapes[0] if single else shapes,
        in_specs=specs,
        out_specs=VMEM if single else [VMEM] * len(shapes),
        scratch_shapes=list(scratch),
        compiler_params=pltpu.CompilerParams(vmem_limit_bytes=room),
        cost_estimate=pl.CostEstimate(flops=1 << 26, bytes_accessed=1 << 20, transcendentals=0),
    )(*args)


def swapped(x):
    return lax.ppermute(x, "core", [(0, 1), (1, 0)])


def exchanged(x, axes):
    return lax.all_to_all(x, axes, 0, 0, tiled=True)


def per_device(factors, onsite, coupling, vectors, quad_weight):
    factor, link, here = factors[0, 0], coupling[0], vectors[0]
    orbitals, columns = here.shape
    rows = link.shape[0]
    quads = lax.axis_size("quad")
    place = jnp.stack([lax.axis_index(a) for a in ("core", "x", "y")]).astype(jnp.int32)
    half_map = (5 * rows, columns)

    leaf = call(
        leaf_kernel,
        [(2, *half_map)],
        [ANY] * 3,
        factor,
        link,
        here,
        scratch=[
            pltpu.VMEM((2, rows, orbitals), BF16),
            pltpu.VMEM((2, rows, orbitals), BF16),
            pltpu.VMEM(link.shape, F32),
            pltpu.VMEM(here.shape, BF16),
            pltpu.SemaphoreType.DMA((6,)),
        ],
    )
    levels = [leaf, swapped(leaf)]
    for axis, make in (("x", leaf_run), ("y", gathered_run)):
        mine = call(
            functools.partial(merge_kernel, make),
            [(lax.axis_size(axis), *half_map)],
            [SMEM, VMEM, VMEM],
            place,
            *levels[-2:],
        )
        own = exchanged(mine, axis)
        levels += [own, swapped(own)]

    share = orbitals // quads
    rows_sent = share + rows // quads
    terms = call(
        down_kernel,
        [(quads, rows_sent, columns)],
        [SMEM, SMEM] + [VMEM] * (3 + len(levels)),
        place,
        quad_weight,
        factor,
        link,
        here,
        *levels,
    )
    spread, subspace = call(
        sum_kernel,
        [(quads, rows_sent, columns), (share, columns)],
        [VMEM],
        exchanged(terms, "quad"),
    )
    field = exchanged(spread, "quad")
    packed = (columns // 2 + 8, columns)
    tiles = call(tile_kernel, [(2, *packed)], [VMEM] * 3, field, onsite[0], link)
    plane = SLAB[:2]
    spread = call(
        pair_kernel,
        [(lax.axis_size(plane), *packed)],
        [SMEM, VMEM],
        place,
        lax.all_gather(tiles, "core"),
    )
    halves = lax.all_gather(jnp.sum(exchanged(spread, plane), axis=0), "core")
    scale = 1.0 / (orbitals * lax.axis_size(SLAB))
    correlation, projected = call(
        functools.partial(final_kernel, scale), [(columns, columns)] * 2, [VMEM], halves
    )
    return subspace[None], correlation, projected


def solution(mesh):
    torus = Mesh(mesh.devices.reshape(mesh.shape["quad"], 4, 4, 2), ("quad", *SLAB))
    return jax.shard_map(
        per_device,
        mesh=torus,
        in_specs=(
            P("quad", SLAB, None, None, None),
            P(SLAB, None, None),
            P(SLAB, None, None),
            P(SLAB, None, None),
            P("quad", None),
        ),
        out_specs=(P(SLAB, "quad", None), P(), P()),
        check_vma=False,
    )
```

time: 164 us -> 160 us (0.976)
  blocking collectives: 76.3 us -> 120 us
  waiting for transfers between devices: 32.8 us -> 6.9 us
  starting transfers between devices: 36.5 us -> 15 us
  local copies, waits for them, and re-layouts: 5.92 us -> 2.99 us
  Pallas kernels: 10.9 us -> 13.4 us
    all_to_all x1 -> x5, blocking collectives: 24.8 us -> 109 us  [exchanged(): return lax.all_to_all(x, axes, 0, 0, tiled=True)]
    all_gather x7 -> x2, blocking collectives: 51.5 us -> 11.3 us  [the longest x1 8 us: per_device(): lax.all_gather(tiles, 'core')]
    all_to_all x2 -> x0, waiting for transfers between devices: 26.1 us -> none  [the longest x1 15.2 us: per_device(): lax.all_to_all(jnp.broadcast_to(summed[None], (quads, *summed.shape)), 'q...]
    all_to_all x2 -> x0, starting transfers between devices: 18.2 us -> none  [the longest x1 11.5 us: per_device(): lax.all_to_all(jnp.broadcast_to(summed[None], (quads, *summed.shape)), 'q...]
    ppermute x4 -> x3, starting transfers between devices: 18.3 us -> 15 us  [swapped(): return lax.ppermute(x, 'core', [(0, 1), (1, 0)])]
    pallas_call x8, Pallas kernels: 10.9 us -> 13.4 us  [call(): pl.pallas_call(kernel, out_shape=shapes[0] if single else shapes, in_spec...]
    broadcast_in_dim x3 -> x0, local copies, waits for them, and re-layouts: 2.21 us -> none  [the longest x1 0.86 us: per_device(): jnp.broadcast_to(mine[None], (count, *packed))]
    ppermute x4 -> x3, waiting for transfers between devices: 6.71 us -> 6.9 us  [swapped(): return lax.ppermute(x, 'core', [(0, 1), (1, 0)])]
  transfers between devices with their start and end apart: 6 -> 3, of which waited for: 6 -> 3; matrix products, arithmetic and copies ran while one was open for 0% -> 0% of each run, Pallas kernels for 0% -> 0%
where the time goes in v2:
time: 160 us; the launch traced here: 159 us
  blocking collectives  120 us (75%)
  starting transfers between devices  15 us (9%)
  Pallas kernels  13.4 us (8%)
  waiting for transfers between devices  6.9 us (4%)
  local copies, waits for them, and re-layouts  2.99 us (2%)
    all_to_all x5, blocking collectives, exchanged(): return lax.all_to_all(x, axes, 0, 0, tiled=True)  109 us
    ppermute x3, starting transfers between devices, swapped(): return lax.ppermute(x, 'core', [(0, 1), (1, 0)])  15 us
    pallas_call x8, Pallas kernels, call(): pl.pallas_call(kernel, out_shape=shapes[0] if single else shapes, in_spec...  13.4 us
    all_gather x1, blocking collectives, per_device(): lax.all_gather(tiles, 'core')  8 us
    ppermute x3, waiting for transfers between devices, swapped(): return lax.ppermute(x, 'core', [(0, 1), (1, 0)])  6.9 us
    all_gather x1, blocking collectives, per_device(): halves = lax.all_gather(jnp.sum(exchanged(spread, plane), axis=0), 'core')  3.28 us
  transfers between devices with their start and end apart: 3, of which 3 were waited for; matrix products, arithmetic and copies ran while one was open for 0% of the time, Pallas kernels for 0%

profile of v2, /device:TPU:1, one launch (start us, length us, event | category | flops | bytes accessed | tf_op | source)
XLA Modules:
  0.0 159.2 jit_solution(12677578245922804283)
XLA Ops:
  0.6 0.0 copy-start
  0.6 1.2 copy-done
  1.9 0.0 copy-start.3
  1.9 0.8 copy-done.3
  2.7 0.0 copy-start.5
  2.7 0.9 copy-done.5
  3.6 1.7 %shard_map.76.own.leaf = f32[2,640,128]{2,1,0:T(8,128)S(1)} custom-call(bf16[2,512,512]{2,1,0:T(8,128)(2,1)S(1)} %bitcast.10, f32[128,128]{1,0:T(8,128)S(1)} %bitcast.13, bf16[512,128]{1,0:T(8,128)(2,1)S(1)} %bitcast.17), custom_call_target="tpu_custom_call" | custom-call | flops 67108864 | bytes 1048576 | tf_op jit(solution)/shard_map/pallas_call | solution.py:256
  5.3 8.7 %collective-permute-start = (f32[2,640,128]{2,1,0:T(8,128)S(1)}, f32[2,640,128]{2,1,0:T(8,128)S(1)}, u32[]{:S(2)}, u32[]{:S(2)}) collective-permute-start(f32[2,640,128]{2,1,0:T(8,128)S(1)} %shard_map.76.own.leaf), channel_id=1, source_target_pairs={{0,1},{1,0},{2,3},{3,2},{4,5},{5,4},{6,7},{7,6},{8,9},{9,8},{10,11... | collective-permute-start | bytes 1966088 | tf_op jit(solution)/shard_map/ppermute | solution.py:268
  14.1 0.1 pad_add_fusion.place
  14.1 1.6 %collective-permute-done.other.leaf_2 = f32[2,640,128]{2,1,0:T(8,128)S(1)} collective-permute-done((f32[2,640,128]{2,1,0:T(8,128)S(1)}, f32[2,640,128]{2,1,0:T(8,128)S(1)}, u32[]{:S(2)}, u32[]{:S(2)}) %collective-permute-start) | collective-permute-done | bytes 655392 | tf_op jit(solution)/shard_map/ppermute | solution.py:268
  15.8 1.2 shard_map.77
  17.0 20.1 %all_to_all.25.own.rank = f32[4,640,128]{2,1,0:T(8,128)S(1)} all-to-all(f32[4,640,128]{2,1,0:T(8,128)S(1)} %shard_map.77), channel_id=1, replica_groups=mesh['quad'=16,'y'=4,'x'=4,'core'=2] {'x'}, dimensions={0} | all-to-all | bytes 2621440 | tf_op jit(solution)/shard_map/all_to_all | solution.py:272
  37.1 3.1 %collective-permute-start.1 = (f32[4,640,128]{2,1,0:T(8,128)S(1)}, f32[4,640,128]{2,1,0:T(8,128)S(1)}, u32[]{:S(2)}, u32[]{:S(2)}) collective-permute-start(f32[4,640,128]{2,1,0:T(8,128)S(1)} %all_to_all.25.own.rank), channel_id=1, source_target_pairs={{0,1},{1,0},{2,3},{3,2},{4,5},{5,4},{6,7},{7,6},{8,9},{9,8},{10,11... | collective-permute-start | bytes 3932168 | tf_op jit(solution)/shard_map/ppermute | solution.py:268
  40.2 2.6 %collective-permute-done.1.other.rank_2 = f32[4,640,128]{2,1,0:T(8,128)S(1)} collective-permute-done((f32[4,640,128]{2,1,0:T(8,128)S(1)}, f32[4,640,128]{2,1,0:T(8,128)S(1)}, u32[]{:S(2)}, u32[]{:S(2)}) %collective-permute-start.1) | collective-permute-done | bytes 1310752 | tf_op jit(solution)/shard_map/ppermute | solution.py:268
  42.8 2.4 %shard_map.78 = f32[4,640,128]{2,1,0:T(8,128)S(1)} custom-call(s32[3]{0:T(128)S(1)} %pad_add_fusion.place, f32[4,640,128]{2,1,0:T(8,128)S(1)} %all_to_all.25.own.rank, f32[4,640,128]{2,1,0:T(8,128)S(1)} %collective-permute-done.1.other.rank_2), custom_call_target="tpu_custom_call" | custom-call | flops 67108864 | bytes 1048576 | tf_op jit(solution)/shard_map/pallas_call | solution.py:256
  45.2 0.0 copy-start.1
  45.2 0.0 copy-start.4
  45.3 0.0 copy-start.6
  45.3 0.0 copy-start.7
  45.3 20.2 %all_to_all.26.file = f32[4,640,128]{2,1,0:T(8,128)S(1)} all-to-all(f32[4,640,128]{2,1,0:T(8,128)S(1)} %shard_map.78), channel_id=1, replica_groups=mesh['quad'=16,'y'=4,'x'=4,'core'=2] {'y'}, dimensions={0} | all-to-all | bytes 2621440 | tf_op jit(solution)/shard_map/all_to_all | solution.py:272
  65.5 3.1 %collective-permute-start.2 = (f32[4,640,128]{2,1,0:T(8,128)S(1)}, f32[4,640,128]{2,1,0:T(8,128)S(1)}, u32[]{:S(2)}, u32[]{:S(2)}) collective-permute-start(f32[4,640,128]{2,1,0:T(8,128)S(1)} %all_to_all.26.file), channel_id=1, source_target_pairs={{0,1},{1,0},{2,3},{3,2},{4,5},{5,4},{6,7},{7,6},{8,9},{9,8},{10,11... | collective-permute-start | bytes 3932168 | tf_op jit(solution)/shard_map/ppermute | solution.py:268
  68.6 2.6 %collective-permute-done.2.file_2 = f32[4,640,128]{2,1,0:T(8,128)S(1)} collective-permute-done((f32[4,640,128]{2,1,0:T(8,128)S(1)}, f32[4,640,128]{2,1,0:T(8,128)S(1)}, u32[]{:S(2)}, u32[]{:S(2)}) %collective-permute-start.2) | collective-permute-done | bytes 1310752 | tf_op jit(solution)/shard_map/ppermute | solution.py:268
  71.3 0.0 copy-done.1
  71.3 0.0 copy-done.4
  71.3 0.0 copy-done.6
  71.3 0.0 copy-done.7
  71.3 5.0 %shard_map.79 = f32[16,40,128]{2,1,0:T(8,128)S(1)} custom-call(s32[3]{0:T(128)S(1)} %pad_add_fusion.place, f32[1,2]{1,0:T(1,128)S(1)} %copy-done.7, bf16[2,512,512]{2,1,0:T(8,128)(2,1)S(1)} %bitcast.11, f32[128,128]{1,0:T(8,128)S(1)} %bitcast.14, bf16[512,128]{1,0:T(8,128)(2,1)S(1)} %bitcast.18, f32[2,640,128]{2,1,0:T(8,128)S(1)} %shard_map.76.own.leaf, ...), custom_call_target="tpu_custom_call" | custom-call | flops 67108864 | bytes 1048576 | tf_op jit(solution)/shard_map/pallas_call | solution.py:256
  76.2 0.0 copy-start.2
  76.2 27.7 %all_to_all.27.terms = f32[16,40,128]{2,1,0:T(8,128)S(1)} all-to-all(f32[16,40,128]{2,1,0:T(8,128)S(1)} %shard_map.79), channel_id=1, replica_groups=mesh['quad'=16,'y'=4,'x'=4,'core'=2] {'quad'}, dimensions={0} | all-to-all | bytes 655360 | tf_op jit(solution)/shard_map/all_to_all | solution.py:272
  103.9 0.6 shard_map.80
  104.6 26.6 %all_to_all.28.field = f32[16,40,128]{2,1,0:T(8,128)S(1)} all-to-all(f32[16,40,128]{2,1,0:T(8,128)S(1)} %get-tuple-element.8), channel_id=1, replica_groups=mesh['quad'=16,'y'=4,'x'=4,'core'=2] {'quad'}, dimensions={0} | all-to-all | bytes 655360 | tf_op jit(solution)/shard_map/all_to_all | solution.py:272
  131.2 0.0 copy-done.2
  131.2 1.2 shard_map.81
  132.4 8.0 %all-gather = f32[4,72,128]{2,1,0:T(8,128)S(1)} all-gather(f32[2,72,128]{2,1,0:T(8,128)S(1)} %shard_map.81), channel_id=2, replica_groups=mesh['quad'=16,'y'=4,'x'=4,'core'=2] {'core'}, dimensions={0}, use_global_device_ids=true | all-gather | bytes 221184 | tf_op jit(solution)/shard_map/all_gather | solution.py:338
  140.4 0.6 shard_map.82
  141.0 14.1 %all_to_all.29 = f32[16,72,128]{2,1,0:T(8,128)S(1)} all-to-all(f32[16,72,128]{2,1,0:T(8,128)S(1)} %shard_map.82), channel_id=1, replica_groups=mesh['quad'=16,'y'=4,'x'=4,'core'=2] {'y','x'}, dimensions={0} | all-to-all | bytes 1179648 | tf_op jit(solution)/shard_map/all_to_all | solution.py:272
  155.1 3.3 %all-gather.1 = f32[144,128]{1,0:T(8,128)S(1)} all-gather(f32[72,128]{1,0:T(8,128)S(1)} %reduce_sum.9), channel_id=3, replica_groups=mesh['quad'=16,'y'=4,'x'=4,'core'=2] {'core'}, dimensions={0}, use_global_device_ids=true | all-gather | bytes 110592 | tf_op jit(solution)/shard_map/all_gather | solution.py:340
  158.4 0.8 shard_map.83
  (1 shorter events, 0.0 us)
Async XLA Ops:
  0.6 1.2 copy-start
  1.9 0.8 copy-start.3
  2.7 0.9 copy-start.5
  5.3 10.5 %collective-permute-start = (f32[2,640,128]{2,1,0:T(8,128)S(1)}, f32[2,640,128]{2,1,0:T(8,128)S(1)}, u32[]{:S(2)}, u32[]{:S(2)}) collective-permute-start(f32[2,640,128]{2,1,0:T(8,128)S(1)} %shard_map.76.own.leaf), channel_id=1, source_target_pairs={{0,1},{1,0},{2,3},{3,2},{4,5},{5,4},{6,7},{7,6},{8,9},{9,8},{10,11... | collective-permute-start | bytes 1966088 | tf_op jit(solution)/shard_map/ppermute | solution.py:268
  37.1 5.8 %collective-permute-start.1 = (f32[4,640,128]{2,1,0:T(8,128)S(1)}, f32[4,640,128]{2,1,0:T(8,128)S(1)}, u32[]{:S(2)}, u32[]{:S(2)}) collective-permute-start(f32[4,640,128]{2,1,0:T(8,128)S(1)} %all_to_all.25.own.rank), channel_id=1, source_target_pairs={{0,1},{1,0},{2,3},{3,2},{4,5},{5,4},{6,7},{7,6},{8,9},{9,8},{10,11... | collective-permute-start | bytes 3932168 | tf_op jit(solution)/shard_map/ppermute | solution.py:268
  45.2 26.0 %copy-start.1 = (bf16[1,1,2,512,512]{4,3,2,1,0:T(8,128)(2,1)S(1)}, bf16[1,1,2,512,512]{4,3,2,1,0:T(8,128)(2,1)}, u32[]{:S(2)}) copy-start(bf16[1,1,2,512,512]{4,3,2,1,0:T(8,128)(2,1)} %param.5) | copy-start | bytes 3145732
  45.2 26.0 %copy-start.4 = (f32[1,128,128]{2,1,0:T(8,128)S(1)}, f32[1,128,128]{2,1,0:T(8,128)}, u32[]{:S(2)}) copy-start(f32[1,128,128]{2,1,0:T(8,128)} %param.7) | copy-start | bytes 196612
  45.3 26.0 %copy-start.6 = (bf16[1,512,128]{2,1,0:T(8,128)(2,1)S(1)}, bf16[1,512,128]{2,1,0:T(8,128)(2,1)}, u32[]{:S(2)}) copy-start(bf16[1,512,128]{2,1,0:T(8,128)(2,1)} %param.8) | copy-start | bytes 393220
  45.3 26.0 %copy-start.7 = (f32[1,2]{1,0:T(1,128)S(1)}, f32[1,2]{1,0:T(1,128)}, u32[]{:S(2)}) copy-start(f32[1,2]{1,0:T(1,128)} %weight.1) | copy-start | bytes 28
  65.5 5.8 %collective-permute-start.2 = (f32[4,640,128]{2,1,0:T(8,128)S(1)}, f32[4,640,128]{2,1,0:T(8,128)S(1)}, u32[]{:S(2)}, u32[]{:S(2)}) collective-permute-start(f32[4,640,128]{2,1,0:T(8,128)S(1)} %all_to_all.26.file), channel_id=1, source_target_pairs={{0,1},{1,0},{2,3},{3,2},{4,5},{5,4},{6,7},{7,6},{8,9},{9,8},{10,11... | collective-permute-start | bytes 3932168 | tf_op jit(solution)/shard_map/ppermute | solution.py:268
  76.2 55.0 %copy-start.2 = (f32[1,512,512]{2,1,0:T(8,128)S(1)}, f32[1,512,512]{2,1,0:T(8,128)}, u32[]{:S(2)}) copy-start(f32[1,512,512]{2,1,0:T(8,128)} %param.6) | copy-start | bytes 3145732

commit v3 on v2

--- a/solution.py
+++ b/solution.py
@@ -29,7 +29,7 @@
 
 def wide(real, imag):
     return tuple(
-        jnp.concatenate([jnp.concatenate([r, -i], 1), jnp.concatenate([i, r], 1)], 0)
+        jnp.concatenate([jnp.concatenate([r, i], 1), jnp.concatenate([-i, r], 1)], 0)
         for r, i in zip(split(real), split(imag))
     )
 
@@ -38,51 +38,52 @@
     def __init__(self, get, count, rows):
         self.get, self.count, self.rows = get, count, rows
 
-    def block(self, half, which, k):
-        n = 2 * self.rows
-        return self.get(half, k)[which * n : (which + 1) * n, :]
-
-    def c_part(self, half, k):
-        return self.get(half, k)[4 * self.rows : 5 * self.rows, :]
-
-    def wide_block(self, which, k):
-        m = self.block(0, which, k)
-        return wide(m[: self.rows], m[self.rows :])
+    def part(self, half, block, k):
+        return self.get(half, k)[block * self.rows : (block + 1) * self.rows, :]
+
+    def state(self, half, which, k):
+        return jnp.concatenate([self.part(half, 2 * which + p, k) for p in (0, 1)], 1)
+
+    def wide(self, which, k):
+        return wide(self.part(0, 2 * which, k), self.part(0, 2 * which + 1, k))
 
     def wide_c(self, k):
-        return wide(self.c_part(0, k), self.c_part(1, k))
+        return wide(self.part(0, 4, k), self.part(1, 4, k))
 
 
 def merged(run, half):
-    states = [run.block(half, 0, 0)]
+    rows, last = run.rows, run.count - 1
+    states = [run.state(half, 0, 0)]
     for k in range(1, run.count):
-        state = times(run.wide_block(0, k), split(states[-1]))
-        states.append(state + run.block(1, 0, k) if half else state)
+        state = times(split(states[-1]), run.wide(0, k))
+        states.append(state + run.state(1, 0, k) if half else state)
 
     def from_left(k):
-        term = times(run.wide_block(1, k), split(states[k - 1]))
-        return term + run.block(1, 1, k) if half else term
-
-    last = run.count - 1
-    back, turn = from_left(last), jnp.concatenate([run.c_part(0, last), run.c_part(1, last)], 0)
-    columns = back.shape[1]
+        term = times(split(states[k - 1]), run.wide(1, k))
+        return term + run.state(1, 1, k) if half else term
+
+    back = from_left(last)
+    turn = jnp.concatenate([run.part(0, 4, last), run.part(1, 4, last)], 1)
+    columns = back.shape[0]
     for k in range(last - 1, 0, -1):
-        both = times(run.wide_c(k), split(jnp.concatenate([back, turn], 1)))
-        back, turn = both[:, :columns] + from_left(k), both[:, columns:]
+        both = times(split(jnp.concatenate([back, turn], 0)), run.wide_c(k))
+        back, turn = both[:columns] + from_left(k), both[columns:]
     first = run.wide_c(0)
-    back = run.block(half, 1, 0) + times(first, split(back))
-    rows = slice(half * run.rows, (half + 1) * run.rows)
-    return states[-1], back, times((first[0][rows], first[1][rows]), split(turn))
+    back = run.state(half, 1, 0) + times(split(back), first)
+    at = slice(half * rows, (half + 1) * rows)
+    turn = times(split(turn), (first[0][:, at], first[1][:, at]))
+    ahead = states[-1]
+    return ahead[:, :rows], ahead[:, rows:], back[:, :rows], back[:, rows:], turn
 
 
 def entering(run, u, t):
     lefts, rights = [u], [t]
     for k in range(run.count - 1):
-        b = run.block(1, 0, k)
-        lefts.append(b if lefts[-1] is None else b + times(run.wide_block(0, k), split(lefts[-1])))
+        b = run.state(1, 0, k)
+        lefts.append(b if lefts[-1] is None else b + times(split(lefts[-1]), run.wide(0, k)))
     for k in range(run.count - 1, 0, -1):
-        term = run.block(1, 1, k) + times(run.wide_block(1, k), split(lefts[k]))
-        rights.append(term if rights[-1] is None else term + times(run.wide_c(k), split(rights[-1])))
+        term = run.state(1, 1, k) + times(split(lefts[k]), run.wide(1, k))
+        rights.append(term if rights[-1] is None else term + times(split(rights[-1]), run.wide_c(k)))
     return lefts, rights[::-1]
 
 
@@ -119,21 +120,23 @@
         )
     for copy in copies:
         copy.start()
-    for copy in copies:
-        copy.wait()
+    copies[0].wait()
     v, v_t = split(link_here[...]), split(link_here[...].T)
+    copies[1].wait()
     y = vectors_here[...]
     for part in (0, 1):
+        copies[2 + 2 * part].wait()
+        copies[3 + 2 * part].wait()
         low, high = tops[part], bottoms[part]
         at = slice(part * rows, (part + 1) * rows)
         left = high[:, :rows]
-        out[0, at, :] = dot(v_t[0], left) + dot(v_t[1], left)
-        out[1, at, :] = times(v_t, split(dot(high, y)))
+        out[0, at, :] = (dot(v_t[0], left) + dot(v_t[1], left)).T
+        out[1, at, :] = times(v_t, split(dot(high, y))).T
         at = slice((2 + part) * rows, (3 + part) * rows)
-        out[0, at, :] = low[:, :rows].astype(F32)
-        out[1, at, :] = dot(low, y)
+        out[0, at, :] = low[:, :rows].astype(F32).T
+        out[1, at, :] = dot(low, y).T
         right = low[:, last:]
-        out[part, 4 * rows :, :] = dot(right, v[0]) + dot(right, v[1])
+        out[part, 4 * rows :, :] = (dot(right, v[0]) + dot(right, v[1])).T
 
 
 def merge_kernel(make, place, own, other, out):
@@ -142,17 +145,16 @@
 
         @pl.when(place[0] == half)
         def _():
-            new_x, new_w, new_c = merged(make(own, other, half, rows), half)
+            blocks = merged(make(own, other, half, rows), half)
             for k in range(out.shape[0]):
-                out[k, : 2 * rows, :] = new_x
-                out[k, 2 * rows : 4 * rows, :] = new_w
-                out[k, 4 * rows :, :] = new_c
+                for n, block in enumerate(blocks):
+                    out[k, n * rows : (n + 1) * rows, :] = block
 
 
 def down_kernel(place, weight, factor, link, vectors, leaf, leaf_2, rank, rank_2, file, file_2, out):
     rows, columns = link.shape
     orbitals = factor.shape[1]
-    zero = jnp.zeros((2 * rows, columns), F32)
+    zero = jnp.zeros((columns, 2 * rows), F32)
 
     def sweep(half):
         lefts, rights = entering(gathered_run(file, file_2, half, rows), None, None)
@@ -162,8 +164,10 @@
         lefts, rights = entering(leaf_run(leaf, leaf_2, half, rows), u, t)
         u, t = lefts[half], rights[half]
         w_re, w_im = weight[0, 0], weight[0, 1]
-        turned = (w_re * u[:rows] - w_im * u[rows:], w_re * u[rows:] + w_im * u[:rows])
-        after = (w_re * t[:rows] - w_im * t[rows:], w_re * t[rows:] + w_im * t[:rows])
+        turned, after = (
+            ((w_re * x[:, :rows] - w_im * x[:, rows:]).T, (w_re * x[:, rows:] + w_im * x[:, :rows]).T)
+            for x in (u, t)
+        )
         v = split(link[...])
         y = vectors[...].astype(F32)
         total = None
@@ -247,7 +251,7 @@
 
 SMEM = pl.BlockSpec(memory_space=pltpu.SMEM)
 VMEM = pl.BlockSpec(memory_space=pltpu.VMEM)
-ANY = pl.BlockSpec(memory_space=pltpu.HBM)
+HBM = pl.BlockSpec(memory_space=pltpu.HBM)
 
 
 def call(kernel, shapes, specs, *args, scratch=(), room=VMEM_BYTES):
@@ -283,10 +287,8 @@
     leaf = call(
         leaf_kernel,
         [(2, *half_map)],
-        [ANY] * 3,
-        factor,
-        link,
-        here,
+        [HBM] * 3,
+        *(pltpu.with_memory_space_constraint(a, pltpu.HBM) for a in (factor, link, here)),
         scratch=[
             pltpu.VMEM((2, rows, orbitals), BF16),
             pltpu.VMEM((2, rows, orbitals), BF16),

time: 160 us -> 156 us (0.975)
  local copies, waits for them, and re-layouts: 2.99 us -> 0.03 us
    unnamed x16 -> x10, local copies, waits for them, and re-layouts: 2.99 us -> 0.03 us
where the time goes in v3:
time: 156 us; the launch traced here: 155 us
  blocking collectives  120 us (77%)
  starting transfers between devices  15 us (10%)
  Pallas kernels  12.4 us (8%)
  waiting for transfers between devices  6.9 us (4%)
    all_to_all x5, blocking collectives, exchanged(): return lax.all_to_all(x, axes, 0, 0, tiled=True)  109 us
    ppermute x3, starting transfers between devices, swapped(): return lax.ppermute(x, 'core', [(0, 1), (1, 0)])  15 us
    pallas_call x8, Pallas kernels, call(): pl.pallas_call(kernel, out_shape=shapes[0] if single else shapes, in_spec...  12.4 us
    all_gather x1, blocking collectives, per_device(): lax.all_gather(tiles, 'core')  8.02 us
    ppermute x3, waiting for transfers between devices, swapped(): return lax.ppermute(x, 'core', [(0, 1), (1, 0)])  6.9 us
    all_gather x1, blocking collectives, per_device(): halves = lax.all_gather(jnp.sum(exchanged(spread, plane), axis=0), 'core')  3.28 us
  transfers between devices with their start and end apart: 3, of which 3 were waited for; matrix products, arithmetic and copies ran while one was open for 0% of the time, Pallas kernels for 0%

profile of v3, /device:TPU:1, one launch (start us, length us, event | category | flops | bytes accessed | tf_op | source)
XLA Modules:
  0.0 155.1 jit_solution(5123433898898797154)
XLA Ops:
  0.6 2.1 %shard_map.76.own.leaf = f32[2,640,128]{2,1,0:T(8,128)S(1)} custom-call(bf16[2,512,512]{2,1,0:T(8,128)(2,1)} %bitcast.10, f32[128,128]{1,0:T(8,128)} %bitcast.13, bf16[512,128]{1,0:T(8,128)(2,1)} %bitcast.17), custom_call_target="tpu_custom_call" | custom-call | flops 67108864 | bytes 1048576 | tf_op jit(solution)/shard_map/pallas_call | solution.py:260
  2.8 8.7 %collective-permute-start = (f32[2,640,128]{2,1,0:T(8,128)S(1)}, f32[2,640,128]{2,1,0:T(8,128)S(1)}, u32[]{:S(2)}, u32[]{:S(2)}) collective-permute-start(f32[2,640,128]{2,1,0:T(8,128)S(1)} %shard_map.76.own.leaf), channel_id=1, source_target_pairs={{0,1},{1,0},{2,3},{3,2},{4,5},{5,4},{6,7},{7,6},{8,9},{9,8},{10,11... | collective-permute-start | bytes 1966088 | tf_op jit(solution)/shard_map/ppermute | solution.py:272
  11.5 0.1 pad_add_fusion.place
  11.6 1.6 %collective-permute-done.other.leaf_2 = f32[2,640,128]{2,1,0:T(8,128)S(1)} collective-permute-done((f32[2,640,128]{2,1,0:T(8,128)S(1)}, f32[2,640,128]{2,1,0:T(8,128)S(1)}, u32[]{:S(2)}, u32[]{:S(2)}) %collective-permute-start) | collective-permute-done | bytes 655392 | tf_op jit(solution)/shard_map/ppermute | solution.py:272
  13.2 1.0 shard_map.77
  14.3 20.1 %all_to_all.25.own.rank = f32[4,640,128]{2,1,0:T(8,128)S(1)} all-to-all(f32[4,640,128]{2,1,0:T(8,128)S(1)} %shard_map.77), channel_id=1, replica_groups=mesh['quad'=16,'y'=4,'x'=4,'core'=2] {'x'}, dimensions={0} | all-to-all | bytes 2621440 | tf_op jit(solution)/shard_map/all_to_all | solution.py:276
  34.3 3.1 %collective-permute-start.1 = (f32[4,640,128]{2,1,0:T(8,128)S(1)}, f32[4,640,128]{2,1,0:T(8,128)S(1)}, u32[]{:S(2)}, u32[]{:S(2)}) collective-permute-start(f32[4,640,128]{2,1,0:T(8,128)S(1)} %all_to_all.25.own.rank), channel_id=1, source_target_pairs={{0,1},{1,0},{2,3},{3,2},{4,5},{5,4},{6,7},{7,6},{8,9},{9,8},{10,11... | collective-permute-start | bytes 3932168 | tf_op jit(solution)/shard_map/ppermute | solution.py:272
  37.5 2.6 %collective-permute-done.1.other.rank_2 = f32[4,640,128]{2,1,0:T(8,128)S(1)} collective-permute-done((f32[4,640,128]{2,1,0:T(8,128)S(1)}, f32[4,640,128]{2,1,0:T(8,128)S(1)}, u32[]{:S(2)}, u32[]{:S(2)}) %collective-permute-start.1) | collective-permute-done | bytes 1310752 | tf_op jit(solution)/shard_map/ppermute | solution.py:272
  40.1 2.2 %shard_map.78 = f32[4,640,128]{2,1,0:T(8,128)S(1)} custom-call(s32[3]{0:T(128)S(1)} %pad_add_fusion.place, f32[4,640,128]{2,1,0:T(8,128)S(1)} %all_to_all.25.own.rank, f32[4,640,128]{2,1,0:T(8,128)S(1)} %collective-permute-done.1.other.rank_2), custom_call_target="tpu_custom_call" | custom-call | flops 67108864 | bytes 1048576 | tf_op jit(solution)/shard_map/pallas_call | solution.py:260
  42.3 0.0 copy-start
  42.3 0.0 copy-start.2
  42.3 0.0 copy-start.3
  42.3 0.0 copy-start.4
  42.3 20.2 %all_to_all.26.file = f32[4,640,128]{2,1,0:T(8,128)S(1)} all-to-all(f32[4,640,128]{2,1,0:T(8,128)S(1)} %shard_map.78), channel_id=1, replica_groups=mesh['quad'=16,'y'=4,'x'=4,'core'=2] {'y'}, dimensions={0} | all-to-all | bytes 2621440 | tf_op jit(solution)/shard_map/all_to_all | solution.py:276
  62.5 3.1 %collective-permute-start.2 = (f32[4,640,128]{2,1,0:T(8,128)S(1)}, f32[4,640,128]{2,1,0:T(8,128)S(1)}, u32[]{:S(2)}, u32[]{:S(2)}) collective-permute-start(f32[4,640,128]{2,1,0:T(8,128)S(1)} %all_to_all.26.file), channel_id=1, source_target_pairs={{0,1},{1,0},{2,3},{3,2},{4,5},{5,4},{6,7},{7,6},{8,9},{9,8},{10,11... | collective-permute-start | bytes 3932168 | tf_op jit(solution)/shard_map/ppermute | solution.py:272
  65.7 2.6 %collective-permute-done.2.file_2 = f32[4,640,128]{2,1,0:T(8,128)S(1)} collective-permute-done((f32[4,640,128]{2,1,0:T(8,128)S(1)}, f32[4,640,128]{2,1,0:T(8,128)S(1)}, u32[]{:S(2)}, u32[]{:S(2)}) %collective-permute-start.2) | collective-permute-done | bytes 1310752 | tf_op jit(solution)/shard_map/ppermute | solution.py:272
  68.3 0.0 copy-done
  68.3 0.0 copy-done.2
  68.3 0.0 copy-done.3
  68.3 0.0 copy-done.4
  68.3 3.9 %shard_map.79 = f32[16,40,128]{2,1,0:T(8,128)S(1)} custom-call(s32[3]{0:T(128)S(1)} %pad_add_fusion.place, f32[1,2]{1,0:T(1,128)S(1)} %copy-done.4, bf16[2,512,512]{2,1,0:T(8,128)(2,1)S(1)} %bitcast.11, f32[128,128]{1,0:T(8,128)S(1)} %bitcast.14, bf16[512,128]{1,0:T(8,128)(2,1)S(1)} %bitcast.18, f32[2,640,128]{2,1,0:T(8,128)S(1)} %shard_map.76.own.leaf, ...), custom_call_target="tpu_custom_call" | custom-call | flops 67108864 | bytes 1048576 | tf_op jit(solution)/shard_map/pallas_call | solution.py:260
  72.2 0.0 copy-start.1
  72.2 27.8 %all_to_all.27.terms = f32[16,40,128]{2,1,0:T(8,128)S(1)} all-to-all(f32[16,40,128]{2,1,0:T(8,128)S(1)} %shard_map.79), channel_id=1, replica_groups=mesh['quad'=16,'y'=4,'x'=4,'core'=2] {'quad'}, dimensions={0} | all-to-all | bytes 655360 | tf_op jit(solution)/shard_map/all_to_all | solution.py:276
  100.0 0.6 shard_map.80
  100.6 26.5 %all_to_all.28.field = f32[16,40,128]{2,1,0:T(8,128)S(1)} all-to-all(f32[16,40,128]{2,1,0:T(8,128)S(1)} %get-tuple-element.8), channel_id=1, replica_groups=mesh['quad'=16,'y'=4,'x'=4,'core'=2] {'quad'}, dimensions={0} | all-to-all | bytes 655360 | tf_op jit(solution)/shard_map/all_to_all | solution.py:276
  127.1 0.0 copy-done.1
  127.1 1.2 shard_map.81
  128.3 8.0 %all-gather = f32[4,72,128]{2,1,0:T(8,128)S(1)} all-gather(f32[2,72,128]{2,1,0:T(8,128)S(1)} %shard_map.81), channel_id=2, replica_groups=mesh['quad'=16,'y'=4,'x'=4,'core'=2] {'core'}, dimensions={0}, use_global_device_ids=true | all-gather | bytes 221184 | tf_op jit(solution)/shard_map/all_gather | solution.py:340
  136.3 0.6 shard_map.82
  136.9 14.1 %all_to_all.29 = f32[16,72,128]{2,1,0:T(8,128)S(1)} all-to-all(f32[16,72,128]{2,1,0:T(8,128)S(1)} %shard_map.82), channel_id=1, replica_groups=mesh['quad'=16,'y'=4,'x'=4,'core'=2] {'y','x'}, dimensions={0} | all-to-all | bytes 1179648 | tf_op jit(solution)/shard_map/all_to_all | solution.py:276
  151.1 3.3 %all-gather.1 = f32[144,128]{1,0:T(8,128)S(1)} all-gather(f32[72,128]{1,0:T(8,128)S(1)} %reduce_sum.9), channel_id=3, replica_groups=mesh['quad'=16,'y'=4,'x'=4,'core'=2] {'core'}, dimensions={0}, use_global_device_ids=true | all-gather | bytes 110592 | tf_op jit(solution)/shard_map/all_gather | solution.py:342
  154.4 0.8 shard_map.83
  (1 shorter events, 0.0 us)
Async XLA Ops:
  2.8 10.5 %collective-permute-start = (f32[2,640,128]{2,1,0:T(8,128)S(1)}, f32[2,640,128]{2,1,0:T(8,128)S(1)}, u32[]{:S(2)}, u32[]{:S(2)}) collective-permute-start(f32[2,640,128]{2,1,0:T(8,128)S(1)} %shard_map.76.own.leaf), channel_id=1, source_target_pairs={{0,1},{1,0},{2,3},{3,2},{4,5},{5,4},{6,7},{7,6},{8,9},{9,8},{10,11... | collective-permute-start | bytes 1966088 | tf_op jit(solution)/shard_map/ppermute | solution.py:272
  34.3 5.8 %collective-permute-start.1 = (f32[4,640,128]{2,1,0:T(8,128)S(1)}, f32[4,640,128]{2,1,0:T(8,128)S(1)}, u32[]{:S(2)}, u32[]{:S(2)}) collective-permute-start(f32[4,640,128]{2,1,0:T(8,128)S(1)} %all_to_all.25.own.rank), channel_id=1, source_target_pairs={{0,1},{1,0},{2,3},{3,2},{4,5},{5,4},{6,7},{7,6},{8,9},{9,8},{10,11... | collective-permute-start | bytes 3932168 | tf_op jit(solution)/shard_map/ppermute | solution.py:272
  42.3 26.0 %copy-start = (bf16[1,1,2,512,512]{4,3,2,1,0:T(8,128)(2,1)S(1)}, bf16[1,1,2,512,512]{4,3,2,1,0:T(8,128)(2,1)}, u32[]{:S(2)}) copy-start(bf16[1,1,2,512,512]{4,3,2,1,0:T(8,128)(2,1)} %param.5) | copy-start | bytes 3145732
  42.3 26.0 %copy-start.2 = (f32[1,128,128]{2,1,0:T(8,128)S(1)}, f32[1,128,128]{2,1,0:T(8,128)}, u32[]{:S(2)}) copy-start(f32[1,128,128]{2,1,0:T(8,128)} %param.7) | copy-start | bytes 196612
  42.3 26.0 %copy-start.3 = (bf16[1,512,128]{2,1,0:T(8,128)(2,1)S(1)}, bf16[1,512,128]{2,1,0:T(8,128)(2,1)}, u32[]{:S(2)}) copy-start(bf16[1,512,128]{2,1,0:T(8,128)(2,1)} %param.8) | copy-start | bytes 393220
  42.3 26.0 %copy-start.4 = (f32[1,2]{1,0:T(1,128)S(1)}, f32[1,2]{1,0:T(1,128)}, u32[]{:S(2)}) copy-start(f32[1,2]{1,0:T(1,128)} %weight.1) | copy-start | bytes 28
  62.5 5.8 %collective-permute-start.2 = (f32[4,640,128]{2,1,0:T(8,128)S(1)}, f32[4,640,128]{2,1,0:T(8,128)S(1)}, u32[]{:S(2)}, u32[]{:S(2)}) collective-permute-start(f32[4,640,128]{2,1,0:T(8,128)S(1)} %all_to_all.26.file), channel_id=1, source_target_pairs={{0,1},{1,0},{2,3},{3,2},{4,5},{5,4},{6,7},{7,6},{8,9},{9,8},{10,11... | collective-permute-start | bytes 3932168 | tf_op jit(solution)/shard_map/ppermute | solution.py:272
  72.2 54.9 %copy-start.1 = (f32[1,512,512]{2,1,0:T(8,128)S(1)}, f32[1,512,512]{2,1,0:T(8,128)}, u32[]{:S(2)}) copy-start(f32[1,512,512]{2,1,0:T(8,128)} %param.6) | copy-start | bytes 3145732

commit v4 on v3

--- a/solution.py
+++ b/solution.py
@@ -151,42 +151,92 @@
                     out[k, n * rows : (n + 1) * rows, :] = block
 
 
-def down_kernel(place, weight, factor, link, vectors, leaf, leaf_2, rank, rank_2, file, file_2, out):
+def base_kernel(weight, factor, vectors, out):
+    y = vectors[...].astype(F32)
+    real, imag = split(weight[0, 0] * y), split(-weight[0, 1] * y)
+    out[...] = (dot(factor[0], real[0]) + dot(factor[0], real[1])) + (
+        dot(factor[1], imag[0]) + dot(factor[1], imag[1])
+    )
+
+
+def inner_kernel(place, leaf, leaf_2, rank, rank_2, out):
+    rows = out.shape[0] // 10
+    one = jnp.where(
+        lax.broadcasted_iota(jnp.int32, (rows, rows), 0) == lax.broadcasted_iota(jnp.int32, (rows, rows), 1),
+        1.0,
+        0.0,
+    )
+    none = jnp.zeros((rows, rows), F32)
+    unit, zero = jnp.concatenate([one, none], 1), jnp.zeros((rows, 2 * rows), F32)
+
+    def stacked(*parts):
+        return jnp.concatenate(parts, 0)
+
+    def build(half):
+        run = gathered_run(rank, rank_2, half, rows)
+        last = run.count - 1
+        lefts = [stacked(unit, zero), stacked(run.state(0, 0, 0), run.state(1, 0, 0))]
+        for k in range(1, last):
+            state = times(split(lefts[-1]), run.wide(0, k))
+            lefts.append(state + stacked(zero, run.state(1, 0, k)))
+        rights = [stacked(zero, zero, unit)]
+        for k in range(last, 0, -1):
+            term = times(split(lefts[k]), run.wide(1, k)) + stacked(zero, run.state(1, 1, k))
+            turn = jnp.concatenate([run.part(0, 4, k), run.part(1, 4, k)], 1)
+            if k == last:
+                rights.append(stacked(term, turn))
+            else:
+                rights.append(times(split(rights[-1]), run.wide_c(k)) + stacked(term, zero))
+        u, t = chosen(lefts, place[1]), chosen(rights[::-1], place[1])
+        pair = leaf_run(leaf, leaf_2, half, rows)
+        mid = times(split(u), pair.wide(0, 0)) + stacked(zero, pair.state(1, 0, 0))
+        if half:
+            u = mid
+        else:
+            term = times(split(mid), pair.wide(1, 1)) + stacked(zero, pair.state(1, 1, 1))
+            t = times(split(t), pair.wide_c(1)) + stacked(term, zero)
+        whole = stacked(u, t)
+        for n in range(5):
+            for p in (0, 1):
+                at = (2 * n + p) * rows
+                out[at : at + rows, :] = whole[n * rows : (n + 1) * rows, p * rows : (p + 1) * rows]
+
+    for half in (0, 1):
+
+        @pl.when(place[0] == half)
+        def _():
+            build(half)
+
+
+def down_kernel(place, weight, factor, link, base, inner, file, file_2, out):
     rows, columns = link.shape
     orbitals = factor.shape[1]
     zero = jnp.zeros((columns, 2 * rows), F32)
 
+    def block(n):
+        return inner[2 * n * rows : (2 * n + 1) * rows, :], inner[(2 * n + 1) * rows : (2 * n + 2) * rows, :]
+
     def sweep(half):
         lefts, rights = entering(gathered_run(file, file_2, half, rows), None, None)
-        u, t = chosen([zero] + lefts[1:], place[2]), chosen(rights[:-1] + [zero], place[2])
-        lefts, rights = entering(gathered_run(rank, rank_2, half, rows), u, t)
-        u, t = chosen(lefts, place[1]), chosen(rights, place[1])
-        lefts, rights = entering(leaf_run(leaf, leaf_2, half, rows), u, t)
-        u, t = lefts[half], rights[half]
+        u = split(chosen([zero] + lefts[1:], place[2]))
+        t = split(chosen(rights[:-1] + [zero], place[2]))
+        t = jnp.concatenate(block(3), 1) + (times(t, wide(*block(4))) + times(u, wide(*block(2))))
+        u = jnp.concatenate(block(1), 1) + times(u, wide(*block(0)))
         w_re, w_im = weight[0, 0], weight[0, 1]
         turned, after = (
             ((w_re * x[:, :rows] - w_im * x[:, rows:]).T, (w_re * x[:, rows:] + w_im * x[:, :rows]).T)
             for x in (u, t)
         )
         v = split(link[...])
-        y = vectors[...].astype(F32)
-        total = None
-        for part, w in ((0, w_re), (1, -w_im)):
-            sign = 1.0 if part == 0 else -1.0
-            field = w * y
-            moved = times(v, split(after[part]))
-            field = jnp.concatenate(
-                [
-                    field[:rows] + sign * turned[part],
-                    field[rows : orbitals - rows],
-                    field[orbitals - rows :] + sign * moved,
-                ],
-                0,
-            )
-            high, low = split(field)
+        total = base[...]
+        for part, sign in ((0, 1.0), (1, -1.0)):
             f = factor[part]
-            term = dot(f, high) + dot(f, low)
-            total = term if total is None else total + term
+            for field, cols in (
+                (turned[part], slice(0, rows)),
+                (times(v, split(after[part])), slice(orbitals - rows, orbitals)),
+            ):
+                high, low = split(sign * field)
+                total = total + (dot(f[:, cols], high) + dot(f[:, cols], low))
         count = out.shape[0]
         share, spare = orbitals // count, rows // count
         for q in range(count):
@@ -311,16 +361,19 @@
 
     share = orbitals // quads
     rows_sent = share + rows // quads
+    base = call(base_kernel, [(orbitals, columns)], [SMEM, VMEM, VMEM], quad_weight, factor, here)
+    inner = call(inner_kernel, [(10 * rows, rows)], [SMEM] + [VMEM] * 4, place, *levels[:4])
     terms = call(
         down_kernel,
         [(quads, rows_sent, columns)],
-        [SMEM, SMEM] + [VMEM] * (3 + len(levels)),
+        [SMEM, SMEM] + [VMEM] * 6,
         place,
         quad_weight,
         factor,
         link,
-        here,
-        *levels,
+        base,
+        inner,
+        *levels[4:],
     )
     spread, subspace = call(
         sum_kernel,

time: 156 us -> 155 us (level)
  waiting for transfers between devices: 6.9 us -> 4.26 us
  Pallas kernels: 12.4 us -> 14.6 us
    ppermute x3, waiting for transfers between devices: 6.9 us -> 4.26 us  [swapped(): return lax.ppermute(x, 'core', [(0, 1), (1, 0)])]
    pallas_call x8 -> x10, Pallas kernels: 12.4 us -> 14.6 us  [call(): pl.pallas_call(kernel, out_shape=shapes[0] if single else shapes, in_spec...]
  transfers between devices with their start and end apart: 3 -> 3, of which waited for: 3 -> 2; matrix products, arithmetic and copies ran while one was open for 0% -> 0% of each run, Pallas kernels for 0% -> 2%
where the time goes in v4:
time: 155 us
  blocking collectives  120 us (77%)
  starting transfers between devices  15 us (10%)
  Pallas kernels  14.6 us (9%)
  waiting for transfers between devices  4.26 us (3%)
    all_to_all x5, blocking collectives, exchanged(): return lax.all_to_all(x, axes, 0, 0, tiled=True)  109 us
    ppermute x3, starting transfers between devices, swapped(): return lax.ppermute(x, 'core', [(0, 1), (1, 0)])  15 us
    pallas_call x10, Pallas kernels, call(): pl.pallas_call(kernel, out_shape=shapes[0] if single else shapes, in_spec...  14.6 us
    all_gather x1, blocking collectives, per_device(): lax.all_gather(tiles, 'core')  8.02 us
    ppermute x3, waiting for transfers between devices, swapped(): return lax.ppermute(x, 'core', [(0, 1), (1, 0)])  4.26 us
    all_gather x1, blocking collectives, per_device(): halves = lax.all_gather(jnp.sum(exchanged(spread, plane), axis=0), 'core')  3.28 us
  transfers between devices with their start and end apart: 3, of which 2 were waited for; matrix products, arithmetic and copies ran while one was open for 0% of the time, Pallas kernels for 2%

profile of v4, /device:TPU:1, one launch (start us, length us, event | category | flops | bytes accessed | tf_op | source)
XLA Modules:
  0.0 154.7 jit_solution(16364048948580735247)
XLA Ops:
  0.6 2.1 %shard_map.77.own.leaf = f32[2,640,128]{2,1,0:T(8,128)S(1)} custom-call(bf16[2,512,512]{2,1,0:T(8,128)(2,1)} %bitcast.10, f32[128,128]{1,0:T(8,128)} %bitcast.14, bf16[512,128]{1,0:T(8,128)(2,1)} %bitcast.18), custom_call_target="tpu_custom_call" | custom-call | flops 67108864 | bytes 1048576 | tf_op jit(solution)/shard_map/pallas_call | solution.py:310
  2.8 8.7 %collective-permute-start = (f32[2,640,128]{2,1,0:T(8,128)S(1)}, f32[2,640,128]{2,1,0:T(8,128)S(1)}, u32[]{:S(2)}, u32[]{:S(2)}) collective-permute-start(f32[2,640,128]{2,1,0:T(8,128)S(1)} %shard_map.77.own.leaf), channel_id=1, source_target_pairs={{0,1},{1,0},{2,3},{3,2},{4,5},{5,4},{6,7},{7,6},{8,9},{9,8},{10,11... | collective-permute-start | bytes 1966088 | tf_op jit(solution)/shard_map/ppermute | solution.py:322
  11.5 0.1 pad_add_fusion.place
  11.6 1.6 %collective-permute-done.other.leaf_2 = f32[2,640,128]{2,1,0:T(8,128)S(1)} collective-permute-done((f32[2,640,128]{2,1,0:T(8,128)S(1)}, f32[2,640,128]{2,1,0:T(8,128)S(1)}, u32[]{:S(2)}, u32[]{:S(2)}) %collective-permute-start) | collective-permute-done | bytes 655392 | tf_op jit(solution)/shard_map/ppermute | solution.py:322
  13.2 1.0 shard_map.78
  14.3 20.1 %all_to_all.25.rank.own = f32[4,640,128]{2,1,0:T(8,128)S(1)} all-to-all(f32[4,640,128]{2,1,0:T(8,128)S(1)} %shard_map.78), channel_id=1, replica_groups=mesh['quad'=16,'y'=4,'x'=4,'core'=2] {'x'}, dimensions={0} | all-to-all | bytes 2621440 | tf_op jit(solution)/shard_map/all_to_all | solution.py:326
  34.3 3.1 %collective-permute-start.1 = (f32[4,640,128]{2,1,0:T(8,128)S(1)}, f32[4,640,128]{2,1,0:T(8,128)S(1)}, u32[]{:S(2)}, u32[]{:S(2)}) collective-permute-start(f32[4,640,128]{2,1,0:T(8,128)S(1)} %all_to_all.25.rank.own), channel_id=1, source_target_pairs={{0,1},{1,0},{2,3},{3,2},{4,5},{5,4},{6,7},{7,6},{8,9},{9,8},{10,11... | collective-permute-start | bytes 3932168 | tf_op jit(solution)/shard_map/ppermute | solution.py:322
  37.5 2.6 %collective-permute-done.1.rank_2.other = f32[4,640,128]{2,1,0:T(8,128)S(1)} collective-permute-done((f32[4,640,128]{2,1,0:T(8,128)S(1)}, f32[4,640,128]{2,1,0:T(8,128)S(1)}, u32[]{:S(2)}, u32[]{:S(2)}) %collective-permute-start.1) | collective-permute-done | bytes 1310752 | tf_op jit(solution)/shard_map/ppermute | solution.py:322
  40.1 2.2 %shard_map.80 = f32[4,640,128]{2,1,0:T(8,128)S(1)} custom-call(s32[3]{0:T(128)S(1)} %pad_add_fusion.place, f32[4,640,128]{2,1,0:T(8,128)S(1)} %all_to_all.25.rank.own, f32[4,640,128]{2,1,0:T(8,128)S(1)} %collective-permute-done.1.rank_2.other), custom_call_target="tpu_custom_call" | custom-call | flops 67108864 | bytes 1048576 | tf_op jit(solution)/shard_map/pallas_call | solution.py:310
  42.3 0.0 copy-start
  42.3 0.0 copy-start.3
  42.3 0.0 copy-start.4
  42.3 20.2 %all_to_all.26.file = f32[4,640,128]{2,1,0:T(8,128)S(1)} all-to-all(f32[4,640,128]{2,1,0:T(8,128)S(1)} %shard_map.80), channel_id=1, replica_groups=mesh['quad'=16,'y'=4,'x'=4,'core'=2] {'y'}, dimensions={0} | all-to-all | bytes 2621440 | tf_op jit(solution)/shard_map/all_to_all | solution.py:326
  62.5 3.1 %collective-permute-start.2 = (f32[4,640,128]{2,1,0:T(8,128)S(1)}, f32[4,640,128]{2,1,0:T(8,128)S(1)}, u32[]{:S(2)}, u32[]{:S(2)}) collective-permute-start(f32[4,640,128]{2,1,0:T(8,128)S(1)} %all_to_all.26.file), channel_id=1, source_target_pairs={{0,1},{1,0},{2,3},{3,2},{4,5},{5,4},{6,7},{7,6},{8,9},{9,8},{10,11... | collective-permute-start | bytes 3932168 | tf_op jit(solution)/shard_map/ppermute | solution.py:322
  65.7 0.0 copy-done
  65.7 0.0 copy-done.3
  65.7 0.0 copy-done.4
  65.7 1.3 shard_map.76.base
  67.0 0.0 copy-start.2
  67.0 2.2 %shard_map.79.inner = f32[1280,128]{1,0:T(8,128)S(1)} custom-call(s32[3]{0:T(128)S(1)} %pad_add_fusion.place, f32[2,640,128]{2,1,0:T(8,128)S(1)} %shard_map.77.own.leaf, f32[2,640,128]{2,1,0:T(8,128)S(1)} %collective-permute-done.other.leaf_2, f32[4,640,128]{2,1,0:T(8,128)S(1)} %all_to_all.25.rank.own, f32[4,640,128]{2,1,0:T(8,128)S(1)} %collective-permute-done.1.rank_2.other), custom_call_target="tpu_custom_call" | custom-call | flops 67108864 | bytes 1048576 | tf_op jit(solution)/shard_map/pallas_call | solution.py:310
  69.1 0.0 collective-permute-done.2.file_2
  69.2 0.0 copy-done.2
  69.2 2.7 %shard_map.81 = f32[16,40,128]{2,1,0:T(8,128)S(1)} custom-call(s32[3]{0:T(128)S(1)} %pad_add_fusion.place, f32[1,2]{1,0:T(1,128)S(1)} %copy-done.4, bf16[2,512,512]{2,1,0:T(8,128)(2,1)S(1)} %bitcast.12, f32[128,128]{1,0:T(8,128)S(1)} %bitcast.15, f32[512,128]{1,0:T(8,128)S(1)} %shard_map.76.base, f32[1280,128]{1,0:T(8,128)S(1)} %shard_map.79.inner, ...), custom_call_target="tpu_custom_call" | custom-call | flops 67108864 | bytes 1048576 | tf_op jit(solution)/shard_map/pallas_call | solution.py:310
  71.8 0.0 copy-start.1
  71.9 27.7 %all_to_all.27.terms = f32[16,40,128]{2,1,0:T(8,128)S(1)} all-to-all(f32[16,40,128]{2,1,0:T(8,128)S(1)} %shard_map.81), channel_id=1, replica_groups=mesh['quad'=16,'y'=4,'x'=4,'core'=2] {'quad'}, dimensions={0} | all-to-all | bytes 655360 | tf_op jit(solution)/shard_map/all_to_all | solution.py:326
  99.6 0.6 shard_map.82
  100.2 26.5 %all_to_all.28.field = f32[16,40,128]{2,1,0:T(8,128)S(1)} all-to-all(f32[16,40,128]{2,1,0:T(8,128)S(1)} %get-tuple-element.8), channel_id=1, replica_groups=mesh['quad'=16,'y'=4,'x'=4,'core'=2] {'quad'}, dimensions={0} | all-to-all | bytes 655360 | tf_op jit(solution)/shard_map/all_to_all | solution.py:326
  126.7 0.0 copy-done.1
  126.7 1.2 shard_map.83
  127.9 8.0 %all-gather = f32[4,72,128]{2,1,0:T(8,128)S(1)} all-gather(f32[2,72,128]{2,1,0:T(8,128)S(1)} %shard_map.83), channel_id=2, replica_groups=mesh['quad'=16,'y'=4,'x'=4,'core'=2] {'core'}, dimensions={0}, use_global_device_ids=true | all-gather | bytes 221184 | tf_op jit(solution)/shard_map/all_gather | solution.py:393
  135.9 0.6 shard_map.84
  136.5 14.1 %all_to_all.29 = f32[16,72,128]{2,1,0:T(8,128)S(1)} all-to-all(f32[16,72,128]{2,1,0:T(8,128)S(1)} %shard_map.84), channel_id=1, replica_groups=mesh['quad'=16,'y'=4,'x'=4,'core'=2] {'y','x'}, dimensions={0} | all-to-all | bytes 1179648 | tf_op jit(solution)/shard_map/all_to_all | solution.py:326
  150.7 3.3 %all-gather.1 = f32[144,128]{1,0:T(8,128)S(1)} all-gather(f32[72,128]{1,0:T(8,128)S(1)} %reduce_sum.9), channel_id=3, replica_groups=mesh['quad'=16,'y'=4,'x'=4,'core'=2] {'core'}, dimensions={0}, use_global_device_ids=true | all-gather | bytes 110592 | tf_op jit(solution)/shard_map/all_gather | solution.py:395
  154.0 0.8 shard_map.85
  (1 shorter events, 0.0 us)
Async XLA Ops:
  2.8 10.5 %collective-permute-start = (f32[2,640,128]{2,1,0:T(8,128)S(1)}, f32[2,640,128]{2,1,0:T(8,128)S(1)}, u32[]{:S(2)}, u32[]{:S(2)}) collective-permute-start(f32[2,640,128]{2,1,0:T(8,128)S(1)} %shard_map.77.own.leaf), channel_id=1, source_target_pairs={{0,1},{1,0},{2,3},{3,2},{4,5},{5,4},{6,7},{7,6},{8,9},{9,8},{10,11... | collective-permute-start | bytes 1966088 | tf_op jit(solution)/shard_map/ppermute | solution.py:322
  34.3 5.8 %collective-permute-start.1 = (f32[4,640,128]{2,1,0:T(8,128)S(1)}, f32[4,640,128]{2,1,0:T(8,128)S(1)}, u32[]{:S(2)}, u32[]{:S(2)}) collective-permute-start(f32[4,640,128]{2,1,0:T(8,128)S(1)} %all_to_all.25.rank.own), channel_id=1, source_target_pairs={{0,1},{1,0},{2,3},{3,2},{4,5},{5,4},{6,7},{7,6},{8,9},{9,8},{10,11... | collective-permute-start | bytes 3932168 | tf_op jit(solution)/shard_map/ppermute | solution.py:322
  42.3 23.4 %copy-start = (bf16[1,1,2,512,512]{4,3,2,1,0:T(8,128)(2,1)S(1)}, bf16[1,1,2,512,512]{4,3,2,1,0:T(8,128)(2,1)}, u32[]{:S(2)}) copy-start(bf16[1,1,2,512,512]{4,3,2,1,0:T(8,128)(2,1)} %param.5) | copy-start | bytes 3145732
  42.3 23.4 %copy-start.3 = (bf16[1,512,128]{2,1,0:T(8,128)(2,1)S(1)}, bf16[1,512,128]{2,1,0:T(8,128)(2,1)}, u32[]{:S(2)}) copy-start(bf16[1,512,128]{2,1,0:T(8,128)(2,1)} %param.8) | copy-start | bytes 393220
  42.3 23.4 %copy-start.4 = (f32[1,2]{1,0:T(1,128)S(1)}, f32[1,2]{1,0:T(1,128)}, u32[]{:S(2)}) copy-start(f32[1,2]{1,0:T(1,128)} %weight.3) | copy-start | bytes 28
  62.5 6.6 %collective-permute-start.2 = (f32[4,640,128]{2,1,0:T(8,128)S(1)}, f32[4,640,128]{2,1,0:T(8,128)S(1)}, u32[]{:S(2)}, u32[]{:S(2)}) collective-permute-start(f32[4,640,128]{2,1,0:T(8,128)S(1)} %all_to_all.26.file), channel_id=1, source_target_pairs={{0,1},{1,0},{2,3},{3,2},{4,5},{5,4},{6,7},{7,6},{8,9},{9,8},{10,11... | collective-permute-start | bytes 3932168 | tf_op jit(solution)/shard_map/ppermute | solution.py:322
  67.0 2.2 %copy-start.2 = (f32[1,128,128]{2,1,0:T(8,128)S(1)}, f32[1,128,128]{2,1,0:T(8,128)}, u32[]{:S(2)}) copy-start(f32[1,128,128]{2,1,0:T(8,128)} %param.7) | copy-start | bytes 196612
  71.8 54.9 %copy-start.1 = (f32[1,512,512]{2,1,0:T(8,128)S(1)}, f32[1,512,512]{2,1,0:T(8,128)}, u32[]{:S(2)}) copy-start(f32[1,512,512]{2,1,0:T(8,128)} %param.6) | copy-start | bytes 3145732

commit v5 on v4

--- a/solution.py
+++ b/solution.py
@@ -159,6 +159,10 @@
     )
 
 
+def halves_kernel(onsite, out):
+    out[0], out[1] = split(0.5 * onsite[...])
+
+
 def inner_kernel(place, leaf, leaf_2, rank, rank_2, out):
     rows = out.shape[0] // 10
     one = jnp.where(
@@ -265,12 +269,12 @@
 
 def tile_kernel(field, onsite, link, out):
     columns = field.shape[2]
-    orbitals, rows = onsite.shape[0], link.shape[0]
+    orbitals, rows = onsite.shape[1], link.shape[0]
     share = orbitals // field.shape[0]
     whole = field[:, :share, :].reshape(orbitals, columns)
     following = field[:, share:, :].reshape(rows, columns)
     parts = split(whole)
-    weighted = 0.5 * times(split(onsite[...]), parts)
+    weighted = times((onsite[0], onsite[1]), parts)
     coupled = times(split(link[...]), split(following))
     weighted = jnp.concatenate([weighted[: orbitals - rows], weighted[orbitals - rows :] + coupled], 0)
     flipped = tuple(p.T for p in parts)
@@ -304,8 +308,8 @@
 HBM = pl.BlockSpec(memory_space=pltpu.HBM)
 
 
-def call(kernel, shapes, specs, *args, scratch=(), room=VMEM_BYTES):
-    shapes = [jax.ShapeDtypeStruct(s, F32) for s in shapes]
+def call(kernel, shapes, specs, *args, scratch=(), room=VMEM_BYTES, dtype=F32):
+    shapes = [jax.ShapeDtypeStruct(s, dtype) for s in shapes]
     single = len(shapes) == 1
     return pl.pallas_call(
         kernel,
@@ -347,6 +351,8 @@
             pltpu.SemaphoreType.DMA((6,)),
         ],
     )
+    base = call(base_kernel, [(orbitals, columns)], [SMEM, VMEM, VMEM], quad_weight, factor, here)
+    onsite_parts = call(halves_kernel, [(2, orbitals, orbitals)], [VMEM], onsite[0], dtype=BF16)
     levels = [leaf, swapped(leaf)]
     for axis, make in (("x", leaf_run), ("y", gathered_run)):
         mine = call(
@@ -358,10 +364,11 @@
         )
         own = exchanged(mine, axis)
         levels += [own, swapped(own)]
+        if axis == "x":
+            levels[-1], base, onsite_parts = lax.optimization_barrier((levels[-1], base, onsite_parts))
 
     share = orbitals // quads
     rows_sent = share + rows // quads
-    base = call(base_kernel, [(orbitals, columns)], [SMEM, VMEM, VMEM], quad_weight, factor, here)
     inner = call(inner_kernel, [(10 * rows, rows)], [SMEM] + [VMEM] * 4, place, *levels[:4])
     terms = call(
         down_kernel,
@@ -383,7 +390,7 @@
     )
     field = exchanged(spread, "quad")
     packed = (columns // 2 + 8, columns)
-    tiles = call(tile_kernel, [(2, *packed)], [VMEM] * 3, field, onsite[0], link)
+    tiles = call(tile_kernel, [(2, *packed)], [VMEM] * 3, field, onsite_parts, link)
     plane = SLAB[:2]
     spread = call(
         pair_kernel,

time: 155 us -> 155 us (level)
    pallas_call x10 -> x11, Pallas kernels: 14.6 us -> 14.8 us  [call(): pl.pallas_call(kernel, out_shape=shapes[0] if single else shapes, in_spec...]
  transfers between devices with their start and end apart: 3 -> 3, of which waited for: 2 -> 3; matrix products, arithmetic and copies ran while one was open for 0% -> 0% of each run, Pallas kernels for 2% -> 2%
where the time goes in v5:
time: 155 us; the launch traced here: 154 us
  blocking collectives  120 us (77%)
  starting transfers between devices  15.3 us (10%)
  Pallas kernels  14.8 us (10%)
  waiting for transfers between devices  3.15 us (2%)
    all_to_all x5, blocking collectives, exchanged(): return lax.all_to_all(x, axes, 0, 0, tiled=True)  109 us
    ppermute x3, starting transfers between devices, swapped(): return lax.ppermute(x, 'core', [(0, 1), (1, 0)])  15.3 us
    pallas_call x11, Pallas kernels, call(): pl.pallas_call(kernel, out_shape=shapes[0] if single else shapes, in_spec...  14.8 us
    all_gather x1, blocking collectives, per_device(): lax.all_gather(tiles, 'core')  8.07 us
    all_gather x1, blocking collectives, per_device(): halves = lax.all_gather(jnp.sum(exchanged(spread, plane), axis=0), 'core')  3.28 us
    ppermute x3, waiting for transfers between devices, swapped(): return lax.ppermute(x, 'core', [(0, 1), (1, 0)])  3.15 us
  transfers between devices with their start and end apart: 3, of which 3 were waited for; matrix products, arithmetic and copies ran while one was open for 0% of the time, Pallas kernels for 2%

profile of v5, /device:TPU:1, one launch (start us, length us, event | category | flops | bytes accessed | tf_op | source)
XLA Modules:
  0.0 154.4 jit_solution(3045594832764583863)
XLA Ops:
  0.6 2.1 %shard_map.76.own.leaf = f32[2,640,128]{2,1,0:T(8,128)S(1)} custom-call(bf16[2,512,512]{2,1,0:T(8,128)(2,1)} %bitcast.10, f32[128,128]{1,0:T(8,128)} %bitcast.14, bf16[512,128]{1,0:T(8,128)(2,1)} %bitcast.18), custom_call_target="tpu_custom_call" | custom-call | flops 67108864 | bytes 1048576 | tf_op jit(solution)/shard_map/pallas_call | solution.py:314
  2.8 8.7 %collective-permute-start = (f32[2,640,128]{2,1,0:T(8,128)S(1)}, f32[2,640,128]{2,1,0:T(8,128)S(1)}, u32[]{:S(2)}, u32[]{:S(2)}) collective-permute-start(f32[2,640,128]{2,1,0:T(8,128)S(1)} %shard_map.76.own.leaf), channel_id=1, source_target_pairs={{0,1},{1,0},{2,3},{3,2},{4,5},{5,4},{6,7},{7,6},{8,9},{9,8},{10,11... | collective-permute-start | bytes 1966088 | tf_op jit(solution)/shard_map/ppermute | solution.py:326
  11.5 0.1 pad_add_fusion.place
  11.6 1.6 %collective-permute-done.other.leaf_2 = f32[2,640,128]{2,1,0:T(8,128)S(1)} collective-permute-done((f32[2,640,128]{2,1,0:T(8,128)S(1)}, f32[2,640,128]{2,1,0:T(8,128)S(1)}, u32[]{:S(2)}, u32[]{:S(2)}) %collective-permute-start) | collective-permute-done | bytes 655392 | tf_op jit(solution)/shard_map/ppermute | solution.py:326
  13.2 1.0 shard_map.77
  14.3 0.0 copy-start
  14.3 0.0 copy-start.3
  14.3 0.0 copy-start.4
  14.3 20.2 %all_to_all.25.rank.own = f32[4,640,128]{2,1,0:T(8,128)S(1)} all-to-all(f32[4,640,128]{2,1,0:T(8,128)S(1)} %shard_map.77), channel_id=1, replica_groups=mesh['quad'=16,'y'=4,'x'=4,'core'=2] {'x'}, dimensions={0} | all-to-all | bytes 2621440 | tf_op jit(solution)/shard_map/all_to_all | solution.py:330
  34.5 0.0 copy-start.1
  34.5 3.3 %collective-permute-start.1 = (f32[4,640,128]{2,1,0:T(8,128)S(1)}, f32[4,640,128]{2,1,0:T(8,128)S(1)}, u32[]{:S(2)}, u32[]{:S(2)}) collective-permute-start(f32[4,640,128]{2,1,0:T(8,128)S(1)} %all_to_all.25.rank.own), channel_id=1, source_target_pairs={{0,1},{1,0},{2,3},{3,2},{4,5},{5,4},{6,7},{7,6},{8,9},{9,8},{10,11... | collective-permute-start | bytes 3932168 | tf_op jit(solution)/shard_map/ppermute | solution.py:326
  37.8 0.0 copy-done
  37.8 0.0 copy-done.3
  37.8 0.0 copy-done.4
  37.8 1.3 shard_map.78.base
  39.1 0.0 copy-done.1
  39.1 0.3 shard_map.79.onsite
  39.3 1.1 collective-permute-done.1.rank_2.other
  40.4 2.2 %shard_map.81 = f32[4,640,128]{2,1,0:T(8,128)S(1)} custom-call(s32[3]{0:T(128)S(1)} %pad_add_fusion.place, f32[4,640,128]{2,1,0:T(8,128)S(1)} %all_to_all.25.rank.own, f32[4,640,128]{2,1,0:T(8,128)S(1)} %collective-permute-done.1.rank_2.other), custom_call_target="tpu_custom_call" | custom-call | flops 67108864 | bytes 1048576 | tf_op jit(solution)/shard_map/pallas_call | solution.py:314
  42.6 20.1 %all_to_all.26.file = f32[4,640,128]{2,1,0:T(8,128)S(1)} all-to-all(f32[4,640,128]{2,1,0:T(8,128)S(1)} %shard_map.81), channel_id=1, replica_groups=mesh['quad'=16,'y'=4,'x'=4,'core'=2] {'y'}, dimensions={0} | all-to-all | bytes 2621440 | tf_op jit(solution)/shard_map/all_to_all | solution.py:330
  62.7 0.0 copy-start.2
  62.7 3.3 %collective-permute-start.2 = (f32[4,640,128]{2,1,0:T(8,128)S(1)}, f32[4,640,128]{2,1,0:T(8,128)S(1)}, u32[]{:S(2)}, u32[]{:S(2)}) collective-permute-start(f32[4,640,128]{2,1,0:T(8,128)S(1)} %all_to_all.26.file), channel_id=1, source_target_pairs={{0,1},{1,0},{2,3},{3,2},{4,5},{5,4},{6,7},{7,6},{8,9},{9,8},{10,11... | collective-permute-start | bytes 3932168 | tf_op jit(solution)/shard_map/ppermute | solution.py:326
  65.9 2.2 %shard_map.80.inner = f32[1280,128]{1,0:T(8,128)S(1)} custom-call(s32[3]{0:T(128)S(1)} %pad_add_fusion.place, f32[2,640,128]{2,1,0:T(8,128)S(1)} %shard_map.76.own.leaf, f32[2,640,128]{2,1,0:T(8,128)S(1)} %collective-permute-done.other.leaf_2, f32[4,640,128]{2,1,0:T(8,128)S(1)} %all_to_all.25.rank.own, f32[4,640,128]{2,1,0:T(8,128)S(1)} %collective-permute-done.1.rank_2.other), custom_call_target="tpu_custom_call" | custom-call | flops 67108864 | bytes 1048576 | tf_op jit(solution)/shard_map/pallas_call | solution.py:314
  68.1 0.5 collective-permute-done.2.file_2
  68.6 0.0 copy-done.2
  68.6 2.7 %shard_map.82 = f32[16,40,128]{2,1,0:T(8,128)S(1)} custom-call(s32[3]{0:T(128)S(1)} %pad_add_fusion.place, f32[1,2]{1,0:T(1,128)S(1)} %copy-done.4, bf16[2,512,512]{2,1,0:T(8,128)(2,1)S(1)} %bitcast.12, f32[128,128]{1,0:T(8,128)S(1)} %bitcast.15, f32[512,128]{1,0:T(8,128)S(1)} %shard_map.78.base, f32[1280,128]{1,0:T(8,128)S(1)} %shard_map.80.inner, ...), custom_call_target="tpu_custom_call" | custom-call | flops 67108864 | bytes 1048576 | tf_op jit(solution)/shard_map/pallas_call | solution.py:314
  71.3 27.7 %all_to_all.27.terms = f32[16,40,128]{2,1,0:T(8,128)S(1)} all-to-all(f32[16,40,128]{2,1,0:T(8,128)S(1)} %shard_map.82), channel_id=1, replica_groups=mesh['quad'=16,'y'=4,'x'=4,'core'=2] {'quad'}, dimensions={0} | all-to-all | bytes 655360 | tf_op jit(solution)/shard_map/all_to_all | solution.py:330
  99.0 0.6 shard_map.83
  99.6 26.7 %all_to_all.28.field = f32[16,40,128]{2,1,0:T(8,128)S(1)} all-to-all(f32[16,40,128]{2,1,0:T(8,128)S(1)} %get-tuple-element.13), channel_id=1, replica_groups=mesh['quad'=16,'y'=4,'x'=4,'core'=2] {'quad'}, dimensions={0} | all-to-all | bytes 655360 | tf_op jit(solution)/shard_map/all_to_all | solution.py:330
  126.3 1.2 shard_map.84
  127.5 8.1 %all-gather = f32[4,72,128]{2,1,0:T(8,128)S(1)} all-gather(f32[2,72,128]{2,1,0:T(8,128)S(1)} %shard_map.84), channel_id=2, replica_groups=mesh['quad'=16,'y'=4,'x'=4,'core'=2] {'core'}, dimensions={0}, use_global_device_ids=true | all-gather | bytes 221184 | tf_op jit(solution)/shard_map/all_gather | solution.py:400
  135.6 0.6 shard_map.85
  136.2 14.1 %all_to_all.29 = f32[16,72,128]{2,1,0:T(8,128)S(1)} all-to-all(f32[16,72,128]{2,1,0:T(8,128)S(1)} %shard_map.85), channel_id=1, replica_groups=mesh['quad'=16,'y'=4,'x'=4,'core'=2] {'y','x'}, dimensions={0} | all-to-all | bytes 1179648 | tf_op jit(solution)/shard_map/all_to_all | solution.py:330
  150.3 3.3 %all-gather.1 = f32[144,128]{1,0:T(8,128)S(1)} all-gather(f32[72,128]{1,0:T(8,128)S(1)} %reduce_sum.9), channel_id=3, replica_groups=mesh['quad'=16,'y'=4,'x'=4,'core'=2] {'core'}, dimensions={0}, use_global_device_ids=true | all-gather | bytes 110592 | tf_op jit(solution)/shard_map/all_gather | solution.py:402
  153.6 0.8 shard_map.86
  (1 shorter events, 0.0 us)
Async XLA Ops:
  2.8 10.5 %collective-permute-start = (f32[2,640,128]{2,1,0:T(8,128)S(1)}, f32[2,640,128]{2,1,0:T(8,128)S(1)}, u32[]{:S(2)}, u32[]{:S(2)}) collective-permute-start(f32[2,640,128]{2,1,0:T(8,128)S(1)} %shard_map.76.own.leaf), channel_id=1, source_target_pairs={{0,1},{1,0},{2,3},{3,2},{4,5},{5,4},{6,7},{7,6},{8,9},{9,8},{10,11... | collective-permute-start | bytes 1966088 | tf_op jit(solution)/shard_map/ppermute | solution.py:326
  14.3 23.5 %copy-start = (bf16[1,1,2,512,512]{4,3,2,1,0:T(8,128)(2,1)S(1)}, bf16[1,1,2,512,512]{4,3,2,1,0:T(8,128)(2,1)}, u32[]{:S(2)}) copy-start(bf16[1,1,2,512,512]{4,3,2,1,0:T(8,128)(2,1)} %param.5) | copy-start | bytes 3145732
  14.3 23.5 %copy-start.3 = (bf16[1,512,128]{2,1,0:T(8,128)(2,1)S(1)}, bf16[1,512,128]{2,1,0:T(8,128)(2,1)}, u32[]{:S(2)}) copy-start(bf16[1,512,128]{2,1,0:T(8,128)(2,1)} %param.8) | copy-start | bytes 393220
  14.3 23.5 %copy-start.4 = (f32[1,2]{1,0:T(1,128)S(1)}, f32[1,2]{1,0:T(1,128)}, u32[]{:S(2)}) copy-start(f32[1,2]{1,0:T(1,128)} %weight.3) | copy-start | bytes 28
  34.5 4.6 %copy-start.1 = (f32[1,512,512]{2,1,0:T(8,128)S(1)}, f32[1,512,512]{2,1,0:T(8,128)}, u32[]{:S(2)}) copy-start(f32[1,512,512]{2,1,0:T(8,128)} %param.6) | copy-start | bytes 3145732
  34.5 5.9 %collective-permute-start.1 = (f32[4,640,128]{2,1,0:T(8,128)S(1)}, f32[4,640,128]{2,1,0:T(8,128)S(1)}, u32[]{:S(2)}, u32[]{:S(2)}) collective-permute-start(f32[4,640,128]{2,1,0:T(8,128)S(1)} %all_to_all.25.rank.own), channel_id=1, source_target_pairs={{0,1},{1,0},{2,3},{3,2},{4,5},{5,4},{6,7},{7,6},{8,9},{9,8},{10,11... | collective-permute-start | bytes 3932168 | tf_op jit(solution)/shard_map/ppermute | solution.py:326
  62.7 5.9 %copy-start.2 = (f32[1,128,128]{2,1,0:T(8,128)S(1)}, f32[1,128,128]{2,1,0:T(8,128)}, u32[]{:S(2)}) copy-start(f32[1,128,128]{2,1,0:T(8,128)} %param.7) | copy-start | bytes 196612
  62.7 5.9 %collective-permute-start.2 = (f32[4,640,128]{2,1,0:T(8,128)S(1)}, f32[4,640,128]{2,1,0:T(8,128)S(1)}, u32[]{:S(2)}, u32[]{:S(2)}) collective-permute-start(f32[4,640,128]{2,1,0:T(8,128)S(1)} %all_to_all.26.file), channel_id=1, source_target_pairs={{0,1},{1,0},{2,3},{3,2},{4,5},{5,4},{6,7},{7,6},{8,9},{9,8},{10,11... | collective-permute-start | bytes 3932168 | tf_op jit(solution)/shard_map/ppermute | solution.py:326
